TPU v7x, 32 devices: a whole 2x2x4 slice. The times are simulated.
32 devices in a mesh: dom: 4 (over y, x), col: 8 (over z, core).
Axes of the slice: x: 2, y: 2, z: 4, core: 2. Of those that a mesh axis runs over, the one named last changes fastest.
Arguments:
- ensemble: float32 [128, 5, 96, 1024], P('dom', None, None, 'col'), may hold values from -6 to 6
- depth_class: int32 [96, 1024], P(None, 'col'), may hold values from 0 to 7
- obs_index: int32 [6144], P('col'), may hold values from 0 to 12287
- obs_value: float32 [6144], P('col'), may hold values from -4 to 16
- annealing_exponents: float32 [96, 1024], P(None, 'col'), may hold values from 0.05 to 1
Outputs:
- posterior: float32 [5, 96, 1024], P(None, None, 'col')
Inputs may be any that keep to these rules, and one draw needn't show every extreme that they name: `obs_index`: each entry is a cell of its own block of 128 columns, numbered row * 128 + column within the block; entries may repeat.
All inputs are finite; a program needn't handle non-finite values.
Results may differ from a plain program's by a relative error of at most 0.0003.
Values sent between devices are 32-bit elements; how exact they have to be, the bound alone decides.
No kernel may reach another device: no remote copies, remote signals or barrier semaphores. Data moves between devices by JAX's collectives and lax.ppermute only.
A program may use at most 128 MiB of HBM per device.

v0:
```python
import jax
import jax.numpy as jnp
from jax import lax
from jax.sharding import PartitionSpec as P

ROW_REACH = 8


TIME_STEP = 0.25
CORIOLIS = 0.2


def with_halo(cells, sides, width):
    for axis, dim in sides:
        count = lax.axis_size(axis)
        head = lax.slice_in_dim(cells, 0, width, axis=dim)
        tail = lax.slice_in_dim(cells, cells.shape[dim] - width, cells.shape[dim], axis=dim)
        cells = jnp.concatenate(
            [
                lax.ppermute(tail, axis, [(i, (i + 1) % count) for i in range(count)]),
                cells,
                lax.ppermute(head, axis, [((i + 1) % count, i) for i in range(count)]),
            ],
            axis=dim,
        )
    return cells


def joined(part, axis, combine):
    gathered = jax.tree.map(lambda a: lax.all_gather(a, axis), part)

    def take(source):
        return jax.tree.map(lambda a: lax.dynamic_index_in_dim(a, source, 0, False), gathered)

    return lax.fori_loop(
        1, lax.axis_size(axis), lambda source, state: combine(state, take(source)), take(0)
    )


def diff_cols(field):
    return 0.5 * (field[..., 2:] - field[..., :-2])


def diff_rows(field):
    padded = jnp.pad(field, [(0, 0)] * (field.ndim - 2) + [(1, 1), (0, 0)])
    return 0.5 * (padded[..., 2:, :] - padded[..., :-2, :])


def integrate_model_ahead(solution_vector, bathymetry_points):
    height = solution_vector[..., 0, :, :]
    zonal_flow = solution_vector[..., 1, :, :]
    meridional = solution_vector[..., 2, :, :]
    tracers = solution_vector[..., 3:, :, :]
    zonal_new = (
        zonal_flow[..., 1:-1]
        - TIME_STEP * diff_cols(height)
        + TIME_STEP * CORIOLIS * meridional[..., 1:-1]
    )
    merid_new = (
        meridional[..., 1:-1]
        - TIME_STEP * diff_rows(height)[..., 1:-1]
        - TIME_STEP * CORIOLIS * zonal_flow[..., 1:-1]
    )
    inner_depth = bathymetry_points[..., 1:-1]
    height_new = height[..., 2:-2] - TIME_STEP * (
        diff_cols(inner_depth * zonal_new) + diff_rows(inner_depth * merid_new)[..., 1:-1]
    )
    tracer_new = tracers[..., 2:-2] - TIME_STEP * (
        zonal_new[..., None, :, 1:-1] * diff_cols(tracers)[..., 1:-1]
        + merid_new[..., None, :, 1:-1] * diff_rows(tracers)[..., 2:-2]
    )
    return jnp.concatenate(
        [
            height_new[..., None, :, :],
            zonal_new[..., None, :, 1:-1],
            merid_new[..., None, :, 1:-1],
            tracer_new,
        ],
        axis=-3,
    )


def smoothing_tables(number_of_meridional_lines, reach, number_of_lateral_lines, radius):
    row_ids = jnp.arange(number_of_meridional_lines).astype(jnp.float32)
    rows_table = jnp.maximum(
        0.0, 1.0 - jnp.abs(row_ids[:, None] - row_ids[None, :]) / (reach + 1.0)
    )
    span_ids = jnp.arange(number_of_lateral_lines + 2 * radius).astype(jnp.float32)
    target_ids = jnp.arange(number_of_lateral_lines).astype(jnp.float32)
    cols_table = jnp.maximum(
        0.0, 1.0 - jnp.abs(span_ids[:, None] - radius - target_ids[None, :]) / (radius + 1.0)
    )
    return (rows_table, cols_table)


def combine_parts(first, second):
    joint = jnp.maximum(first[0], second[0])
    scale_first = jnp.exp(first[0] - joint)
    scale_second = jnp.exp(second[0] - joint)
    return (
        joint,
        first[1] * scale_first + second[1] * scale_second,
        first[2] * scale_first[None] + second[2] * scale_second[None],
    )


def on_device(ensemble, depth_class, obs_index, obs_value, annealing_exponents):
    ensemble_solutions, fields, number_of_meridional_lines, number_of_lateral_lines = ensemble.shape
    radius = number_of_lateral_lines // 2
    bathymetry_points = (0.5 + 0.25 * depth_class.astype(jnp.float32)).reshape(
        1, 1, number_of_meridional_lines, number_of_lateral_lines
    )
    enlarged_array, bathymetry_broadened = (
        with_halo(ensemble, (("col", 3),), 2),
        with_halo(bathymetry_points, (("col", 3),), 2),
    )
    halfway_solution = integrate_model_ahead(enlarged_array, bathymetry_broadened[0, 0])
    bordered_solution_array = with_halo(halfway_solution, (("col", 3),), 2)
    prior_solution = integrate_model_ahead(bordered_solution_array, bathymetry_broadened[0, 0])
    rows_table, cols_table = smoothing_tables(
        number_of_meridional_lines, ROW_REACH, number_of_lateral_lines, radius
    )
    surface_elevation = prior_solution[:, 0].reshape(
        ensemble_solutions, number_of_meridional_lines * number_of_lateral_lines
    )
    prognosed_solution = surface_elevation[:, obs_index]
    misfit = obs_value[None, :] - prognosed_solution
    loss_terms = -0.5 * misfit * misfit
    loglik = (
        jnp.zeros(
            (ensemble_solutions, number_of_meridional_lines * number_of_lateral_lines), jnp.float32
        )
        .at[:, obs_index]
        .add(loss_terms)
        .reshape(ensemble_solutions, number_of_meridional_lines, number_of_lateral_lines)
    )
    smoothed = jnp.einsum("ij,mjc->mic", rows_table, loglik, precision=lax.Precision.HIGHEST)
    widened_misfit = with_halo(smoothed, (("col", 2),), radius)
    filtered_lateral_lines = jnp.einsum(
        "mrk,kc->mrc", widened_misfit, cols_table, precision=lax.Precision.HIGHEST
    )
    logarithmic_importance = annealing_exponents[None] * filtered_lateral_lines
    local_peak = jnp.max(logarithmic_importance, axis=0)
    sample_importance = jnp.exp(logarithmic_importance - local_peak[None])
    combined = joined(
        (
            local_peak,
            jnp.sum(sample_importance, axis=0),
            jnp.sum(sample_importance[:, None] * prior_solution, axis=0),
        ),
        "dom",
        combine_parts,
    )
    posterior = combined[2] / combined[1][None]
    return posterior


def solution(mesh):
    in_specs = (P("dom", None, None, "col"), P(None, "col"), P("col"), P("col"), P(None, "col"))
    out_specs = P(None, None, "col")
    return jax.shard_map(
        on_device, mesh=mesh, in_specs=in_specs, out_specs=out_specs, check_vma=False
    )
```

profile of v0, /device:TPU:0, one launch (start us, length us, event | category | flops | bytes accessed | tf_op | source)
XLA Modules:
  0.0 207.9 jit_solution(2363490642260108674)
XLA Ops:
  0.0 10.6 %copy.32 = f32[32,5,96,128]{2,0,3,1:T(8,128)} copy(f32[32,5,96,128]{3,2,1,0:T(8,128)} %param.7) | data formatting | bytes 15728640 | tf_op args[0]
  10.6 1.0 fusion.99
  11.6 0.6 collective-permute-start
  12.2 4.1 %collective-permute-start.1 = (f32[32,5,96,2]{2,0,3,1:T(8,128)S(1)}, f32[32,5,96,2]{2,0,3,1:T(8,128)S(1)}, u32[]{:S(2)}, u32[]{:S(2)}) collective-permute-start(f32[32,5,96,2]{2,0,3,1:T(8,128)S(1)} %get-tuple-element.221), channel_id=1, source_target_pairs={{1,0},{2,1},{3,2},{4,3},{5,4},{6,5},{7,6},{0,7},{9,8},{10,9},{11,1... | collective-permute-start | bytes 368648 | tf_op jit(solution)/shard_map/ppermute | solution.py:22
  16.4 3.5 %collective-permute-start.3 = (f32[1,1,96,2]{3,2,1,0:T(8,128)S(1)}, f32[1,1,96,2]{3,2,1,0:T(8,128)S(1)}, u32[]{:S(2)}, u32[]{:S(2)}) collective-permute-start(f32[1,1,96,2]{3,2,1,0:T(8,128)S(1)} %get-tuple-element.249), channel_id=1, source_target_pairs={{1,0},{2,1},{3,2},{4,3},{5,4},{6,5},{7,6},{0,7},{9,8},{10,9},{11,1... | collective-permute-start | bytes 2312 | tf_op jit(solution)/shard_map/ppermute | solution.py:22
  19.9 2.3 %collective-permute-done.2 = f32[1,1,96,2]{3,2,1,0:T(8,128)S(1)} collective-permute-done((f32[1,1,96,2]{3,2,1,0:T(8,128)S(1)}, f32[1,1,96,2]{3,2,1,0:T(8,128)S(1)}, u32[]{:S(2)}, u32[]{:S(2)}) %collective-permute-start.2) | collective-permute-done | bytes 800 | tf_op jit(solution)/shard_map/ppermute | solution.py:20
  22.5 3.6 %maximum_bitcast_fusion.3 = (f32[32,96,132]{1,0,2:T(8,128)S(1)}, f32[32,96,132]{1,0,2:T(8,128)S(1)}, f32[32,96,132]{1,0,2:T(8,128)S(1)}) fusion(f32[32,5,96,2]{2,0,3,1:T(8,128)S(1)} %collective-permute-done.1, f32[32,5,96,128]{2,0,3,1:T(8,128)} %copy.32, f32[32,5,96,2]{2,0,3,1:T(8,128)S(1)} %collective-permute-done), kind=kLoop, calls=%fused_computation.61 | loop fusion | flops 2433024 | bytes 12976128 | tf_op jit(solution)/shard_map/squeeze | solution.py:52
  26.2 1.2 pad_slice_fusion.3
  27.4 3.9 %broadcast_multiply_fusion.3 = (f32[32,96,130]{1,0,2:T(8,128)}, f32[32,96,130]{1,0,2:T(8,128)}, f32[32,96,130]{1,0,2:T(8,128)S(1)}, f32[32,96,130]{1,0,2:T(8,128)}) fusion(f32[96,130]{0,1:T(8,128)S(1)} %copy.35, f32[32,96,132]{1,0,2:T(8,128)S(1)} %get-tuple-element.215, f32[32,96,132]{1,0,2:T(8,128)S(1)} %get-tuple-element.217, ...), kind=kLoop, calls=%fused_computation.111 | loop fusion | flops 5191680 | bytes 16024320 | tf_op jit(solution)/shard_map/mul | solution.py:66
  31.3 3.1 %pad_slice_fusion.7 = (f32[32,96,130]{1,0,2:T(8,128)}, f32[32,96,130]{1,0,2:T(8,128)}) fusion(f32[32,96,130]{1,0,2:T(8,128)S(1)} %get-tuple-element.224), kind=kLoop, calls=%fused_computation.104 | loop fusion | bytes 4792320 | tf_op jit(solution)/shard_map/slice | solution.py:46
  34.4 1.2 select_maximum_fusion.5
  35.6 4.9 %fusion.101 = (f32[32,2,96,132]{2,0,3,1:T(8,128)}, f32[32,2,96,132]{2,0,3,1:T(8,128)}) fusion(f32[32,2,98,132]{2,0,3,1:T(8,128)S(1)} %select_maximum_fusion.5), kind=kLoop, calls=%fused_computation.167 | loop fusion | bytes 12976128 | tf_op jit(solution)/shard_map/slice | solution.py:46
  40.5 5.4 %slice_bitcast_fusion.2 = (f32[32,1,96,128]{2,0,3,1:T(8,128)S(1)}, f32[32,96,128]{1,0,2:T(8,128)}, f32[32,96,128]{1,0,2:T(8,128)}, f32[32,1,96,128]{2,0,3,1:T(8,128)S(1)}) fusion(f32[32,96,130]{1,0,2:T(8,128)} %get-tuple-element.225, f32[32,96,130]{1,0,2:T(8,128)} %get-tuple-element.209), kind=kLoop, calls=%fused_computation.162 | loop fusion | bytes 9437184 | tf_op jit(solution)/shard_map/broadcast_in_dim | solution.py:76
  45.9 2.4 %fusion.52 = f32[32,1,96,128]{2,0,3,1:T(8,128)} fusion(f32[32,96,130]{1,0,2:T(8,128)S(1)} %copy-done.11, f32[32,96,130]{1,0,2:T(8,128)S(1)} %copy-done.10, f32[32,96,130]{1,0,2:T(8,128)S(1)} %copy-done.8, f32[32,96,132]{1,0,2:T(8,128)S(1)} %get-tuple-element.217), kind=kLoop, calls=%fused_computation.94 | loop fusion | flops 2752512 | bytes 9437184 | tf_op jit(solution)/shard_map/broadcast_in_dim | solution.py:74
  48.3 5.9 %fusion.17 = f32[32,2,96,128]{2,0,3,1:T(8,128)S(1)} fusion(f32[32,2,96,132]{2,0,3,1:T(8,128)} %get-tuple-element.229, f32[32,2,96,132]{2,0,3,1:T(8,128)} %get-tuple-element.228, f32[32,5,96,2]{2,0,3,1:T(8,128)S(1)} %collective-permute-done.1, f32[32,5,96,128]{2,0,3,1:T(8,128)S(1)} %bitcast.71, f32[32,5,96,2]{2,0,3,1:T(8,128)S(1)} %collective-permute-done, ...), kind=kLoop, calls=%fused_computation.44 | loop fusion | flops 8650752 | bytes 27590656 | tf_op jit(solution)/shard_map/sub | solution.py:68
  54.3 0.9 pad_maximum_fusion.13
  55.2 1.1 copy-done
  56.3 3.5 %collective-permute-start.5 = (f32[32,5,96,2]{2,0,3,1:T(8,128)S(1)}, f32[32,5,96,2]{2,0,3,1:T(8,128)S(1)}, u32[]{:S(2)}, u32[]{:S(2)}) collective-permute-start(f32[32,5,96,2]{2,0,3,1:T(8,128)S(1)} %get-tuple-element.219), channel_id=1, source_target_pairs={{1,0},{2,1},{3,2},{4,3},{5,4},{6,5},{7,6},{0,7},{9,8},{10,9},{11,1... | collective-permute-start | bytes 368648 | tf_op jit(solution)/shard_map/ppermute | solution.py:22
  59.8 4.6 %collective-permute-done.4 = f32[32,5,96,2]{2,0,3,1:T(8,128)S(1)} collective-permute-done((f32[32,5,96,2]{2,0,3,1:T(8,128)S(1)}, f32[32,5,96,2]{2,0,3,1:T(8,128)S(1)}, u32[]{:S(2)}, u32[]{:S(2)}) %collective-permute-start.4) | collective-permute-done | bytes 122912 | tf_op jit(solution)/shard_map/ppermute | solution.py:20
  64.4 4.3 %select_maximum_fusion = f32[32,2,98,132]{2,0,3,1:T(8,128)S(1)} fusion(f32[32,5,96,2]{2,0,3,1:T(8,128)S(1)} %collective-permute-done.5, f32[32,5,96,2]{2,0,3,1:T(8,128)S(1)} %collective-permute-done.4, f32[32,2,96,128]{2,0,3,1:T(8,128)} %copy-done, f32[32,1,96,128]{2,0,3,1:T(8,128)S(1)} %get-tuple-element.244, f32[32,1,96,128]{2,0,3,1:T(8,128)} %copy-done.2, ...), kind=kLoop, calls=%fused_computation.14 | loop fusion | flops 11590656 | bytes 11421696 | tf_op jit(solution)/shard_map/concatenate | solution.py:18
  68.7 5.4 %fusion.100 = (f32[32,2,96,132]{2,0,3,1:T(8,128)}, f32[32,2,96,132]{2,0,3,1:T(8,128)}) fusion(f32[32,2,98,132]{2,0,3,1:T(8,128)S(1)} %select_maximum_fusion), kind=kLoop, calls=%fused_computation.166 | loop fusion | bytes 12976128 | tf_op jit(solution)/shard_map/slice | solution.py:46
  74.4 1.9 maximum_bitcast_fusion
  76.3 1.2 pad_slice_fusion.1
  77.9 1.7 broadcast_multiply_fusion.1
  79.6 2.7 %slice_bitcast_fusion.1 = (f32[32,1,96,128]{2,0,3,1:T(8,128)}, f32[32,96,128]{1,0,2:T(8,128)}) fusion(f32[32,96,130]{1,0,2:T(8,128)S(1)} %get-tuple-element.205), kind=kLoop, calls=%fused_computation.161 | loop fusion | bytes 4718592 | tf_op jit(solution)/shard_map/broadcast_in_dim | solution.py:75
  82.3 2.7 %slice_bitcast_fusion = (f32[32,1,96,128]{2,0,3,1:T(8,128)}, f32[32,96,128]{1,0,2:T(8,128)}) fusion(f32[32,96,130]{1,0,2:T(8,128)S(1)} %get-tuple-element.223), kind=kLoop, calls=%fused_computation.160 | loop fusion | bytes 4718592 | tf_op jit(solution)/shard_map/broadcast_in_dim | solution.py:76
  85.0 1.2 pad_slice_fusion.5
  86.2 2.4 %fusion.46 = f32[32,96,128]{1,0,2:T(8,128)} fusion(f32[32,96,130]{1,0,2:T(8,128)S(1)} %get-tuple-element.239, f32[32,96,130]{1,0,2:T(8,128)S(1)} %get-tuple-element.238, f32[32,96,130]{1,0,2:T(8,128)S(1)} %get-tuple-element.204, f32[32,96,132]{1,0,2:T(8,128)S(1)} %get-tuple-element.214), kind=kLoop, calls=%fused_computation.86 | loop fusion | flops 2752512 | bytes 9437184 | tf_op jit(solution)/shard_map/sub | solution.py:65
  88.6 5.5 %copy.39 = f32[32,96,128]{0,2,1:T(8,128)} copy(f32[32,96,128]{1,0,2:T(8,128)} %fusion.46) | data formatting | bytes 3145728 | tf_op jit(solution)/shard_map/sub | solution.py:65
  94.0 23.2 %scatter_custom_fusion = f32[32,12288]{0,1:T(8,128)} fusion(s32[768]{0:T(1024)S(1)} %compare_select_fusion, f32[]{:T(128)} %constant.83.clone.1, f32[768]{0:T(1024)S(1)} %copy-done.14, f32[]{:T(128)} %constant.89.clone.1, f32[32,12288]{0,1:T(8,128)} %bitcast.72, s32[1024]{0:T(1024)S(1)} %pad_clamp_fusion), kind=kCustom, calls=%fused_computation.56 | custom fusion | flops 98304 | bytes 3153928 | tf_op jit(solution)/shard_map/scatter-add | solution.py:134
  117.3 5.7 %copy.40 = f32[32,96,128]{2,1,0:T(8,128)} copy(f32[32,96,128]{0,2,1:T(8,128)} %bitcast.73) | data formatting | bytes 3145728 | tf_op jit(solution)/shard_map/reshape | solution.py:135
  123.0 2.9 %convolution_bitcast_fusion = f32[32,96,128]{2,1,0:T(8,128)S(1)} fusion(f32[32,96,128]{2,1,0:T(8,128)} %copy.40, f32[96]{0:T(128)S(1)} %iota_convert_fusion.1), kind=kOutput, calls=%fused_computation.107 | convolution fusion | flops 453030912 | bytes 3146112 | tf_op jit(solution)/shard_map/ij,mjc->mic/dot_general | solution.py:137
  125.9 2.2 %fusion.102 = (f32[32,96,64]{2,1,0:T(8,128)}, f32[32,96,64]{2,1,0:T(8,128)}) fusion(f32[32,96,128]{2,1,0:T(8,128)S(1)} %convolution_bitcast_fusion), kind=kLoop, calls=%fused_computation.168 | loop fusion | bytes 3145728 | tf_op jit(solution)/shard_map/slice | solution.py:17
  128.2 1.9 copy.41
  130.1 2.9 %copy.42 = f32[32,96,64]{1,2,0:T(8,128)} copy(f32[32,96,64]{2,1,0:T(8,128)} %get-tuple-element.247) | data formatting | bytes 1572864 | tf_op jit(solution)/shard_map/slice | solution.py:16
  133.0 3.5 %collective-permute-start.7 = (f32[32,96,64]{1,2,0:T(8,128)}, f32[32,96,64]{1,2,0:T(8,128)}, u32[]{:S(2)}, u32[]{:S(2)}) collective-permute-start(f32[32,96,64]{1,2,0:T(8,128)} %copy.42), channel_id=1, source_target_pairs={{1,0},{2,1},{3,2},{4,3},{5,4},{6,5},{7,6},{0,7},{9,8},{10,9},{11,1... | collective-permute-start | bytes 2359304 | tf_op jit(solution)/shard_map/ppermute | solution.py:22
  136.5 11.4 %fusion.9 = f32[32,2,96,128]{2,0,3,1:T(8,128)} fusion(f32[32,2,96,128]{2,0,3,1:T(8,128)} %copy-done, f32[32,2,96,132]{2,0,3,1:T(8,128)} %get-tuple-element.227, f32[32,2,96,132]{2,0,3,1:T(8,128)} %get-tuple-element.226, f32[32,5,96,2]{2,0,3,1:T(8,128)S(1)} %collective-permute-done.5, f32[32,5,96,2]{2,0,3,1:T(8,128)S(1)} %collective-permute-done.4, ...), kind=kLoop, calls=%fused_computation.27 | loop fusion | flops 13369344 | bytes 20692992 | tf_op jit(solution)/shard_map/sub | solution.py:68
  147.9 7.4 %collective-permute-done.6 = f32[32,96,64]{1,2,0:T(8,128)} collective-permute-done((f32[32,96,64]{1,2,0:T(8,128)S(1)}, f32[32,96,64]{1,2,0:T(8,128)}, u32[]{:S(2)}, u32[]{:S(2)}) %collective-permute-start.6) | collective-permute-done | bytes 786464 | tf_op jit(solution)/shard_map/ppermute | solution.py:20
  155.3 1.7 copy.43
  157.0 2.9 %copy.44 = f32[32,96,64]{2,1,0:T(8,128)} copy(f32[32,96,64]{1,2,0:T(8,128)} %collective-permute-done.7) | data formatting | bytes 1572864 | tf_op jit(solution)/shard_map/ppermute | solution.py:22
  159.9 4.5 %fusion.104 = (f32[96,128]{1,0:T(8,128)S(1)}, f32[32,96,128]{2,1,0:T(8,128)S(1)}) fusion(f32[128]{0:T(128)S(1)} %iota_convert_fusion, f32[256]{0:T(256)S(1)} %convert_add_fusion, f32[32,96,64]{2,1,0:T(8,128)} %copy.44, f32[32,96,128]{2,1,0:T(8,128)S(1)} %copy-done.6, f32[32,96,64]{2,1,0:T(8,128)S(1)} %copy.43, f32[96,128]{1,0:T(8,128)S(1)} %copy-done.12), kind=kOutput, calls=%fused_computation.170 | convolution fusion | flops 1210470400 | bytes 4818432 | tf_op jit(solution)/shard_map/mrk,kc->mrc/dot_general | solution.py:139
  164.4 9.4 %all-gather = f32[384,128]{1,0:T(8,128)S(1)} all-gather(f32[96,128]{1,0:T(8,128)S(1)} %get-tuple-element.250), channel_id=2, replica_groups=mesh['dom'=4,'col'=8] {'dom'}, dimensions={0}, use_global_device_ids=true | all-gather | bytes 245760 | tf_op jit(solution)/shard_map/all_gather | solution.py:30
  173.8 1.4 fusion.94
  175.2 3.1 %copy.45 = f32[32,96,128]{1,0,2:T(8,128)} copy(f32[32,96,128]{2,1,0:T(8,128)} %get-tuple-element.203) | data formatting | bytes 3145728 | tf_op jit(solution)/shard_map/exp | solution.py:144
  178.4 6.9 %fusion.3 = f32[5,96,128]{1,2,0:T(8,128)S(1)} fusion(f32[32,2,96,128]{2,0,3,1:T(8,128)} %fusion.9, f32[32,1,96,128]{2,0,3,1:T(8,128)} %get-tuple-element.236, f32[32,1,96,128]{2,0,3,1:T(8,128)} %get-tuple-element.234, f32[32,1,96,128]{2,0,3,1:T(8,128)S(1)} %bitcast.74, f32[32,96,128]{1,0,2:T(8,128)} %copy.45), kind=kLoop, calls=%fused_computation.11 | loop fusion | flops 9768960 | bytes 9682944 | tf_op jit(solution)/shard_map/reduce_sum | solution.py:149
  185.4 12.6 %all-gather.2 = f32[20,96,128]{2,1,0:T(8,128)S(1)} all-gather(f32[5,96,128]{2,1,0:T(8,128)S(1)} %copy.46), channel_id=4, replica_groups=mesh['dom'=4,'col'=8] {'dom'}, dimensions={0}, use_global_device_ids=true | all-gather | bytes 1228800 | tf_op jit(solution)/shard_map/all_gather | solution.py:30
  198.1 8.6 %all-gather.1 = f32[384,128]{1,0:T(8,128)S(1)} all-gather(f32[96,128]{1,0:T(8,128)S(1)} %get-tuple-element.202), channel_id=3, replica_groups=mesh['dom'=4,'col'=8] {'dom'}, dimensions={0}, use_global_device_ids=true | all-gather | bytes 245760 | tf_op jit(solution)/shard_map/all_gather | solution.py:30
  207.2 0.7 broadcast_divide_fusion
  (67 shorter events, 2.3 us)
Async XLA Ops:
  0.0 16.3 %copy-start.13 = (s32[96,128]{1,0:T(8,128)S(1)}, s32[96,128]{1,0:T(8,128)}, u32[]{:S(2)}) copy-start(s32[96,128]{1,0:T(8,128)} %param.8) | copy-start | bytes 147460
  0.0 19.9 %copy-start.15 = (s32[768]{0:T(1024)S(1)}, s32[768]{0:T(1024)}, u32[]{:S(2)}) copy-start(s32[768]{0:T(1024)} %param.9) | copy-start | bytes 9220
  11.6 10.9 %collective-permute-start = (f32[32,5,96,2]{2,0,3,1:T(8,128)S(1)}, f32[32,5,96,2]{2,0,3,1:T(8,128)S(1)}, u32[]{:S(2)}, u32[]{:S(2)}) collective-permute-start(f32[32,5,96,2]{2,0,3,1:T(8,128)S(1)} %get-tuple-element.220), channel_id=1, source_target_pairs={{0,1},{1,2},{2,3},{3,4},{4,5},{5,6},{6,7},{7,0},{8,9},{9,10},{10,1... | collective-permute-start | bytes 368648 | tf_op jit(solution)/shard_map/ppermute | solution.py:20
  12.2 10.3 %collective-permute-start.1 = (f32[32,5,96,2]{2,0,3,1:T(8,128)S(1)}, f32[32,5,96,2]{2,0,3,1:T(8,128)S(1)}, u32[]{:S(2)}, u32[]{:S(2)}) collective-permute-start(f32[32,5,96,2]{2,0,3,1:T(8,128)S(1)} %get-tuple-element.221), channel_id=1, source_target_pairs={{1,0},{2,1},{3,2},{4,3},{5,4},{6,5},{7,6},{0,7},{9,8},{10,9},{11,1... | collective-permute-start | bytes 368648 | tf_op jit(solution)/shard_map/ppermute | solution.py:22
  16.4 5.8 %collective-permute-start.2 = (f32[1,1,96,2]{3,2,1,0:T(8,128)S(1)}, f32[1,1,96,2]{3,2,1,0:T(8,128)S(1)}, u32[]{:S(2)}, u32[]{:S(2)}) collective-permute-start(f32[1,1,96,2]{3,2,1,0:T(8,128)S(1)} %get-tuple-element.248), channel_id=1, source_target_pairs={{0,1},{1,2},{2,3},{3,4},{4,5},{5,6},{6,7},{7,0},{8,9},{9,10},{10,1... | collective-permute-start | bytes 2312 | tf_op jit(solution)/shard_map/ppermute | solution.py:20
  16.4 5.8 %collective-permute-start.3 = (f32[1,1,96,2]{3,2,1,0:T(8,128)S(1)}, f32[1,1,96,2]{3,2,1,0:T(8,128)S(1)}, u32[]{:S(2)}, u32[]{:S(2)}) collective-permute-start(f32[1,1,96,2]{3,2,1,0:T(8,128)S(1)} %get-tuple-element.249), channel_id=1, source_target_pairs={{1,0},{2,1},{3,2},{4,3},{5,4},{6,5},{7,6},{0,7},{9,8},{10,9},{11,1... | collective-permute-start | bytes 2312 | tf_op jit(solution)/shard_map/ppermute | solution.py:22
  26.2 8.2 %slice-start = ((s8[10485760]{0:T(1024)(128)(4,1)}), s8[4194304]{0:T(1024)(128)(4,1)S(1)}, s32[]{:S(2)}) async-start(s8[10485760]{0:T(1024)(128)(4,1)} %bitcast.70), calls=%async_computation | async-start | bytes 8388608
  27.4 7.0 %slice-start.1 = ((s8[10485760]{0:T(1024)(128)(4,1)}), s8[4194304]{0:T(1024)(128)(4,1)S(1)}, s32[]{:S(2)}) async-start(s8[10485760]{0:T(1024)(128)(4,1)} %bitcast.70), calls=%async_computation.1 | async-start | bytes 8388608
  27.4 7.0 %slice-start.2 = ((s8[10485760]{0:T(1024)(128)(4,1)}), s8[2097152]{0:T(1024)(128)(4,1)S(1)}, s32[]{:S(2)}) async-start(s8[10485760]{0:T(1024)(128)(4,1)} %bitcast.70), calls=%async_computation.2 | async-start | bytes 4194304
  40.5 5.4 %copy-start.8 = (f32[32,96,130]{1,0,2:T(8,128)S(1)}, f32[32,96,130]{1,0,2:T(8,128)}, u32[]{:S(2)}) copy-start(f32[32,96,130]{1,0,2:T(8,128)} %get-tuple-element.208) | copy-start | bytes 4792324
  40.5 5.4 %copy-start.10 = (f32[32,96,130]{1,0,2:T(8,128)S(1)}, f32[32,96,130]{1,0,2:T(8,128)}, u32[]{:S(2)}) copy-start(f32[32,96,130]{1,0,2:T(8,128)} %get-tuple-element.240) | copy-start | bytes 4792324
  40.5 5.4 %copy-start.11 = (f32[32,96,130]{1,0,2:T(8,128)S(1)}, f32[32,96,130]{1,0,2:T(8,128)}, u32[]{:S(2)}) copy-start(f32[32,96,130]{1,0,2:T(8,128)} %get-tuple-element.241) | copy-start | bytes 4792324
  45.9 8.4 %copy-start.2 = (f32[32,1,96,128]{2,0,3,1:T(8,128)}, f32[32,1,96,128]{2,0,3,1:T(8,128)S(1)}, u32[]{:S(2)}) copy-start(f32[32,1,96,128]{2,0,3,1:T(8,128)S(1)} %get-tuple-element.253) | copy-start | bytes 4718596
  54.3 2.0 copy-start
  56.3 8.1 %collective-permute-start.4 = (f32[32,5,96,2]{2,0,3,1:T(8,128)S(1)}, f32[32,5,96,2]{2,0,3,1:T(8,128)S(1)}, u32[]{:S(2)}, u32[]{:S(2)}) collective-permute-start(f32[32,5,96,2]{2,0,3,1:T(8,128)S(1)} %get-tuple-element.218), channel_id=1, source_target_pairs={{0,1},{1,2},{2,3},{3,4},{4,5},{5,6},{6,7},{7,0},{8,9},{9,10},{10,1... | collective-permute-start | bytes 368648 | tf_op jit(solution)/shard_map/ppermute | solution.py:20
  56.3 8.1 %collective-permute-start.5 = (f32[32,5,96,2]{2,0,3,1:T(8,128)S(1)}, f32[32,5,96,2]{2,0,3,1:T(8,128)S(1)}, u32[]{:S(2)}, u32[]{:S(2)}) collective-permute-start(f32[32,5,96,2]{2,0,3,1:T(8,128)S(1)} %get-tuple-element.219), channel_id=1, source_target_pairs={{1,0},{2,1},{3,2},{4,3},{5,4},{6,5},{7,6},{0,7},{9,8},{10,9},{11,1... | collective-permute-start | bytes 368648 | tf_op jit(solution)/shard_map/ppermute | solution.py:22
  68.7 5.4 %copy-start.1 = (f32[32,2,96,128]{2,0,3,1:T(8,128)S(1)}, f32[32,2,96,128]{2,0,3,1:T(8,128)}, u32[]{:S(2)}) copy-start(f32[32,2,96,128]{2,0,3,1:T(8,128)} %copy-done) | copy-start | bytes 9437188
  68.7 5.4 %copy-start.3 = (f32[32,1,96,128]{2,0,3,1:T(8,128)S(1)}, f32[32,1,96,128]{2,0,3,1:T(8,128)}, u32[]{:S(2)}) copy-start(f32[32,1,96,128]{2,0,3,1:T(8,128)} %copy-done.2) | copy-start | bytes 4718596
  68.7 5.6 %copy-start.4 = (f32[32,1,96,128]{2,0,3,1:T(8,128)S(1)}, f32[32,1,96,128]{2,0,3,1:T(8,128)}, u32[]{:S(2)}) copy-start(f32[32,1,96,128]{2,0,3,1:T(8,128)} %fusion.52) | copy-start | bytes 4718596
  76.3 1.6 copy-start.9
  88.6 5.5 %copy-start.14 = (f32[768]{0:T(1024)S(1)}, f32[768]{0:T(1024)}, u32[]{:S(2)}) copy-start(f32[768]{0:T(1024)} %param.10) | copy-start | bytes 9220
  125.9 2.2 %copy-start.5 = (f32[32,96,128]{2,1,0:T(8,128)}, f32[32,96,128]{2,1,0:T(8,128)S(1)}, u32[]{:S(2)}) copy-start(f32[32,96,128]{2,1,0:T(8,128)S(1)} %convolution_bitcast_fusion) | copy-start | bytes 4718596
  130.0 25.3 %collective-permute-start.6 = (f32[32,96,64]{1,2,0:T(8,128)S(1)}, f32[32,96,64]{1,2,0:T(8,128)}, u32[]{:S(2)}, u32[]{:S(2)}) collective-permute-start(f32[32,96,64]{1,2,0:T(8,128)S(1)} %copy.41), channel_id=1, source_target_pairs={{0,1},{1,2},{2,3},{3,4},{4,5},{5,6},{6,7},{7,0},{8,9},{9,10},{10,1... | collective-permute-start | bytes 2359304 | tf_op jit(solution)/shard_map/ppermute | solution.py:20
  133.0 24.1 %collective-permute-start.7 = (f32[32,96,64]{1,2,0:T(8,128)}, f32[32,96,64]{1,2,0:T(8,128)}, u32[]{:S(2)}, u32[]{:S(2)}) collective-permute-start(f32[32,96,64]{1,2,0:T(8,128)} %copy.42), channel_id=1, source_target_pairs={{1,0},{2,1},{3,2},{4,3},{5,4},{6,5},{7,6},{0,7},{9,8},{10,9},{11,1... | collective-permute-start | bytes 2359304 | tf_op jit(solution)/shard_map/ppermute | solution.py:22
  147.9 12.0 %copy-start.6 = (f32[32,96,128]{2,1,0:T(8,128)S(1)}, f32[32,96,128]{2,1,0:T(8,128)}, u32[]{:S(2)}) copy-start(f32[32,96,128]{2,1,0:T(8,128)} %copy-done.5) | copy-start | bytes 4718596
  147.9 12.0 %copy-start.12 = (f32[96,128]{1,0:T(8,128)S(1)}, f32[96,128]{1,0:T(8,128)}, u32[]{:S(2)}) copy-start(f32[96,128]{1,0:T(8,128)} %param.11) | copy-start | bytes 147460
  175.2 3.1 %copy-start.7 = (f32[32,96,128]{1,0,2:T(8,128)S(1)}, f32[32,96,128]{1,0,2:T(8,128)}, u32[]{:S(2)}) copy-start(f32[32,96,128]{1,0,2:T(8,128)} %fusion.46) | copy-start | bytes 4718596
where the time goes:
time: 209 us; the launch traced here: 208 us
  other arithmetic  72.4 us (35%)
  local copies, waits for them, and re-layouts  67.4 us (32%)
  blocking collectives  30.6 us (15%)
  starting transfers between devices  15.3 us (7%)
  waiting for transfers between devices  14.3 us (7%)
  matrix products  7.46 us (4%)
    all_gather x3, blocking collectives, joined(): gathered = jax.tree.map(lambda a: lax.all_gather(a, axis), part)  30.6 us
    scatter-add x1, other arithmetic, on_device(): loglik = jnp.zeros((ensemble_solutions, number_of_meridional_lines * numb...  23.2 us
    sub x2, other arithmetic, integrate_model_ahead(): tracers[..., 2:-2]  17.3 us
    slice x6, local copies, waits for them, and re-layouts, diff_rows(): return 0.5 * (padded[..., 2:, :] - padded[..., :-2, :])  16.9 us
    ppermute x4, starting transfers between devices, with_halo(): lax.ppermute(head, axis, [((i + 1) % count, i) for i in range(count)])  14.7 us
    ppermute x4, waiting for transfers between devices, with_halo(): lax.ppermute(tail, axis, [(i, (i + 1) % count) for i in range(count)])  14.3 us
    unnamed x39, local copies, waits for them, and re-layouts  12.4 us
    broadcast_in_dim x2, local copies, waits for them, and re-layouts, integrate_model_ahead(): merid_new[..., None, :, 1:-1]  8.13 us
  transfers between devices with their start and end apart: 8, of which 3 were waited for; matrix products, arithmetic and copies ran while one was open for 8% of the time, Pallas kernels for 0%

commit v1 on v0

v1 whole, which is shorter than its diff:
```python
import functools

import jax
import jax.numpy as jnp
from jax import lax
from jax.experimental import pallas as pl
from jax.experimental.pallas import tpu as pltpu
from jax.sharding import PartitionSpec as P

ROW_REACH = 8
TIME_STEP = 0.25
CORIOLIS = 0.2
GROUP = 16
EDGE = 4
HALF = 8
VMEM = pl.BlockSpec(memory_space=pltpu.VMEM)
ANY = pl.BlockSpec(memory_space=pl.ANY)
PARAMS = pltpu.CompilerParams(vmem_limit_bytes=56 * 1024 * 1024)
f32 = jnp.float32
bf16 = jnp.bfloat16


def depth_of(cls):
    return 0.5 + 0.25 * cls.astype(f32)


def lanes_of(shape):
    return lax.broadcasted_iota(jnp.int32, shape, len(shape) - 1)


def roll_lanes(x, shift):
    return pltpu.roll(x, shift % x.shape[-1] if isinstance(shift, int) else shift, x.ndim - 1)


def step(fields, depth, first, last):
    h, u, v, a, b = fields
    rows = h.shape[0]

    def cols(q):
        return roll_lanes(q, -1) - roll_lanes(q, 1)

    def rws(q):
        return jnp.where(last, 0.0, pltpu.roll(q, rows - 1, 0)) - jnp.where(first, 0.0, pltpu.roll(q, 1, 0))

    half = 0.5 * TIME_STEP
    un = u - half * cols(h) + TIME_STEP * CORIOLIS * v
    vn = v - half * rws(h) - TIME_STEP * CORIOLIS * u
    hn = h - half * (cols(depth * un) + rws(depth * vn))
    an = a - half * (un * cols(a) + vn * rws(a))
    bn = b - half * (un * cols(b) + vn * rws(b))
    return hn, un, vn, an, bn


def two_steps(fields, depth):
    rid = lax.broadcasted_iota(jnp.int32, depth.shape, 0)
    first, last = rid == 0, rid == depth.shape[0] - 1
    return step(step(fields, depth, first, last), depth, first, last)


def pack_kernel(x_hbm, cls_ref, idx_ref, g_ref, pa_ref, pb_ref, buf, sem):
    members, fields, rows, cols = x_hbm.shape
    per = cols // GROUP
    planes = members // per
    even = lax.rem(lax.axis_index("col"), 2) == 0
    copies = [pltpu.make_async_copy(x_hbm.at[:, f], buf.at[f], sem.at[f]) for f in range(fields)]
    for c in copies:
        c.start()

    lane = lanes_of((8, cols))
    grp = lane // GROUP
    sub = (lane % GROUP) // EDGE
    jj = lane % EDGE

    def put(plane, t, right, left):
        at = pl.ds(plane * rows + t * 8, 8)
        pa_ref[at, :] = jnp.where(even, right, left)
        pb_ref[at, :] = jnp.where(even, left, right)

    def edges(f, t):
        at = pl.ds(t * 8, 8)
        right = left = None
        for q in range(planes):
            acc = None
            for i in range(per):
                r = roll_lanes(buf[f, q * per + i, at, :], GROUP * i + HALF)
                acc = r if acc is None else jnp.where(grp == i, r, acc)
            g_ref[q, f, at, :] = acc
            r = roll_lanes(acc, EDGE * q - EDGE)
            l = roll_lanes(acc, EDGE * q - HALF)
            right = r if right is None else jnp.where(sub == q, r, right)
            left = l if left is None else jnp.where(sub == q, l, left)
        return right, left

    for f in range(3):
        copies[f].wait()

        def body(t, carry, f=f):
            right, left = edges(f, t)
            if f == 1:
                d = depth_of(cls_ref[pl.ds(t * 8, 8), :])
                for n in range(3):
                    e = roll_lanes(d, 3 * n + 3)
                    right = jnp.where(lane == EDGE * n, e, right)
                    left = jnp.where(lane == EDGE * n + 3, e, left)
            put(f, t, right, left)
            return carry

        lax.fori_loop(0, rows // 8, body, 0)
    copies[3].wait()
    copies[4].wait()

    def tracers(t, carry):
        ra, la = edges(3, t)
        rb, lb = edges(4, t)
        put(3, t, jnp.where(jj >= 2, ra, roll_lanes(rb, -2)), jnp.where(jj < 2, la, roll_lanes(lb, 2)))
        return carry

    lax.fori_loop(0, rows // 8, tracers, 0)
    n = idx_ref.shape[0]
    for ref in (pa_ref, pb_ref):
        ref[4 * rows : 4 * rows + 8, :] = jnp.zeros((8, cols), f32)
        ref[4 * rows : 4 * rows + n, :] = idx_ref[...].astype(f32)


def forecast_kernel(x_ref, cls_ref, o_ref):
    depth = depth_of(cls_ref[...])

    def body(m, carry):
        out = two_steps([x_ref[m, f] for f in range(5)], depth)
        for f in range(5):
            o_ref[m, f] = out[f]
        return carry

    lax.fori_loop(0, x_ref.shape[0], body, 0)


def pieces_of(x):
    hi = x.astype(bf16)
    rest = x - hi.astype(f32)
    mid = rest.astype(bf16)
    lo = (rest - mid.astype(f32)).astype(bf16)
    return hi, mid, lo


def row_vector(x):
    return jnp.concatenate([x[i : i + 1, :] for i in range(x.shape[0])], axis=1)


def edge_kernel(ra_ref, rb_ref, g_ref, cls_ref, x_hbm, idx_ref, obs_ref, z_ref, loss_ref, hbuf, xs, lhs, low, prod, sem):
    members, _, rows, cols = x_hbm.shape
    per = cols // GROUP
    planes = members // per
    even = lax.rem(lax.axis_index("col"), 2) == 0
    copy = pltpu.make_async_copy(x_hbm.at[:, 0], hbuf, sem)
    copy.start()
    lane = lanes_of((rows, cols))
    j = lane % GROUP
    grp = lane // GROUP

    def received(plane):
        at = slice(plane * rows, (plane + 1) * rows)
        a, b = ra_ref[at, :], rb_ref[at, :]
        return jnp.where(even, b, a), jnp.where(even, a, b)

    depth = depth_of(cls_ref[...])
    tiled = None
    for i in range(per):
        r = roll_lanes(depth, GROUP * i + HALF)
        tiled = r if tiled is None else jnp.where(grp == i, r, tiled)
    ul, ur = received(1)
    dl = roll_lanes(tiled, -EDGE)
    dr = tiled
    for n in range(3):
        dl = jnp.where(j == n + 1, jnp.broadcast_to(ul[:, EDGE * n : EDGE * n + 1], dl.shape), dl)
        dr = jnp.where(j == HALF + n, jnp.broadcast_to(ur[:, EDGE * n + 3 : EDGE * n + 4], dr.shape), dr)
    xs[0, 5] = dl
    xs[1, 5] = dr
    for f in range(5):
        left, right = received(min(f, 3))
        if f == 4:
            left, right = roll_lanes(left, 2), roll_lanes(right, -2)
        xs[0, f] = left
        xs[1, f] = right

    def strips(q, carry):
        left = []
        right = []
        for f in range(5):
            g = g_ref[q, f]
            hl = pltpu.roll(xs[0, f], lax.rem(cols - EDGE * q, cols), 1)
            hr = pltpu.roll(xs[1, f], lax.rem(cols + HALF - EDGE * q, cols), 1)
            left.append(jnp.where(j < EDGE, hl, roll_lanes(g, -EDGE)))
            right.append(jnp.where(j >= HALF, hr, g))
        left = two_steps(left, xs[0, 5])
        right = two_steps(right, xs[1, 5])
        inner = (j >= EDGE) & (j < 2 * EDGE)
        for f in range(5):
            z_ref[q, f] = jnp.where(inner, right[f], roll_lanes(left[f], EDGE))
        return carry

    lax.fori_loop(0, planes, strips, 0)

    idx = row_vector(idx_ref[...])
    obs = row_vector(obs_ref[...])
    nobs = idx.shape[1]
    row, col = lax.shift_right_logical(idx, cols.bit_length() - 1), idx & (cols - 1)
    pick = (lax.broadcasted_iota(jnp.int32, (cols, nobs), 0) == col).astype(f32).astype(bf16)
    pick2 = jnp.concatenate([pick, pick], axis=0)
    isrow = lax.broadcasted_iota(jnp.int32, (rows, nobs), 0) == row
    border = (lane < EDGE) | (lane >= cols - EDGE)
    copy.wait()

    def gather(q, carry):
        for i in range(per):
            at = slice(i * rows, (i + 1) * rows)
            h = jnp.where(border, roll_lanes(z_ref[q, 0], cols - HALF - GROUP * i), hbuf[q * per + i])
            hi, mid, lo = pieces_of(h)
            lhs[at, :cols] = hi
            lhs[at, cols:] = mid
            low[at, :] = lo
        prod[...] = jnp.dot(lhs[...], pick2, preferred_element_type=f32) + jnp.dot(
            low[...], pick, preferred_element_type=f32
        )
        ys = [
            jnp.sum(jnp.where(isrow, prod[i * rows : (i + 1) * rows, :], 0.0), axis=0, keepdims=True)
            for i in range(per)
        ]
        misfit = obs - jnp.concatenate(ys, axis=0)
        loss_ref[pl.ds(pl.multiple_of(q * per, 8), per), :] = -0.5 * misfit * misfit
        return carry

    lax.fori_loop(0, planes, gather, 0)


def spread(losses, indices, offsets, radius, cols, rows, lhs, rhs):
    members = losses[0].shape[0]
    start = 0
    for loss, idx, offset in zip(losses, indices, offsets):
        n = idx.shape[1]
        at = slice(start, start + n)
        start += n
        row, col = lax.shift_right_logical(idx, cols.bit_length() - 1), idx & (cols - 1)
        dist = jnp.abs(lax.broadcasted_iota(jnp.int32, (cols, n), 0) - (col + offset))
        table = jnp.maximum(0, radius + 1 - dist).astype(f32)
        block = lax.shift_right_logical(row, 4)
        for b in range(rows // 16):
            rhs[b * cols : (b + 1) * cols, at] = jnp.where(block == b, table, 0.0).astype(bf16)
        isrow = lax.broadcasted_iota(jnp.int32, (16, n), 0) == (row & 15)
        parts = [p.astype(f32) for p in pieces_of(loss)]
        for m in range(members):
            for p in range(3):
                lhs[p, 16 * m : 16 * m + 16, at] = jnp.where(isrow, parts[p][m : m + 1, :], 0.0).astype(bf16)
    dims = (((1,), (1,)), ((), ()))
    return sum(lax.dot_general(lhs[p], rhs[...], dims, preferred_element_type=f32) for p in range(3))


def own_kernel(loss_ref, idx_ref, o_ref, lhs, rhs, *, radius, cols, rows):
    o_ref[...] = spread([loss_ref[...]], [row_vector(idx_ref[...])], [0], radius, cols, rows, lhs, rhs)


def weigh_kernel(own_ref, la_ref, lb_ref, ra_ref, rb_ref, x_hbm, z_ref, ann_ref, *rest, radius, parts):
    outs = rest[:parts]
    lhs, rhs, acc, logw, tot, xbuf, sem = rest[parts:]
    members, fields, rows, cols = x_hbm.shape
    per = cols // GROUP
    planes = members // per
    copy = pltpu.make_async_copy(x_hbm, xbuf, sem)
    copy.start()
    even = lax.rem(lax.axis_index("col"), 2) == 0
    nrow = la_ref.shape[1] // cols
    at = slice(4 * rows, 4 * rows + nrow)
    ia = row_vector(ra_ref[at, :]).astype(jnp.int32)
    ib = row_vector(rb_ref[at, :]).astype(jnp.int32)
    oa = jnp.where(even, cols, -cols)
    acc[...] = own_ref[...] + spread(
        [la_ref[...], lb_ref[...]], [ia, ib], [oa, -oa], radius, cols, rows, lhs, rhs
    )

    pad = jnp.zeros((ROW_REACH, cols), f32)
    total_rows = rows + 2 * ROW_REACH

    def box(q, sign):
        def sh(x, s):
            return pltpu.roll(x, (total_rows - s) if sign > 0 else s, 0)

        out, width = q, 1
        while 2 * width <= ROW_REACH + 1:
            out = out + sh(out, width)
            width *= 2
        while width < ROW_REACH + 1:
            out = out + sh(q, width)
            width += 1
        return out

    scale = ann_ref[...] * (1.0 / ((ROW_REACH + 1) * (radius + 1)))

    def smooth(m, peak):
        at = pl.ds(pl.multiple_of(m * 16, 16), 16)
        q = jnp.concatenate(
            [pad] + [acc[at, b * cols : (b + 1) * cols] for b in range(rows // 16)] + [pad], axis=0
        )
        w = scale * box(box(q, 1), -1)[ROW_REACH : ROW_REACH + rows, :]
        logw[m] = w
        return jnp.maximum(peak, w)

    peak = lax.fori_loop(0, members, smooth, jnp.full((rows, cols), -jnp.inf, f32))
    tot[fields + 1] = peak
    copy.wait()
    lane = lanes_of((8, cols))
    border = (lane < EDGE) | (lane >= cols - EDGE)

    def sums(t, carry):
        at = pl.ds(pl.multiple_of(t * 8, 8), 8)
        top = tot[fields + 1, at, :]
        total = jnp.zeros((8, cols), f32)
        s = [jnp.zeros((8, cols), f32)] * fields
        for m in range(members):
            q, i = divmod(m, per)
            w = jnp.exp(logw[m, at, :] - top)
            total = total + w
            for f in range(fields):
                x = jnp.where(
                    border, roll_lanes(z_ref[q, f, at, :], cols - HALF - GROUP * i), xbuf[m, f, at, :]
                )
                s[f] = s[f] + w * x
        for f in range(fields):
            tot[f, at, :] = s[f]
        tot[fields, at, :] = total
        return carry

    lax.fori_loop(0, rows // 8, sums, 0)
    part = rows // parts
    me = lax.axis_index("dom")
    for k, ref in enumerate(outs):
        start = pl.multiple_of(partner(me, k, parts) * part, 8)
        ref[...] = tot[:, pl.ds(start, part), :]


def partner(me, k, count):
    return me ^ k if count & (count - 1) == 0 else lax.rem(me + k, count)


def swap(x, k, count):
    return lax.ppermute(x, "dom", [(i, i ^ k if count & (count - 1) == 0 else (i + k) % count) for i in range(count)])


def join_kernel(*refs):
    *ins, out = refs
    fields = out.shape[0]
    peak = functools.reduce(jnp.maximum, [r[fields + 1] for r in ins])
    total = 0.0
    s = [0.0] * fields
    for r in ins:
        e = jnp.exp(r[fields + 1] - peak)
        total = total + r[fields] * e
        for f in range(fields):
            s[f] = s[f] + r[f] * e
    for f in range(fields):
        out[f] = s[f] / total


def place_kernel(*refs):
    *ins, out = refs
    part = ins[0].shape[1]
    me = lax.axis_index("dom")
    count = len(ins)
    for k, r in enumerate(ins):
        source = me if k == 0 else (me ^ k if count & (count - 1) == 0 else lax.rem(me - k + count, count))
        out[:, pl.ds(pl.multiple_of(source * part, 8), part), :] = r[...]


def on_device(ensemble, depth_class, obs_index, obs_value, annealing_exponents):
    members, fields, rows, cols = ensemble.shape
    radius = cols // 2
    per = cols // GROUP
    planes = members // per
    nobs = obs_index.shape[0]
    ncol = lax.axis_size("col")
    ndom = lax.axis_size("dom")
    S = jax.ShapeDtypeStruct
    idx = obs_index.reshape(nobs // cols, cols)
    obs = obs_value.reshape(nobs // cols, cols)

    payload = S((4 * rows + 8, cols), f32)
    packed, pa, pb = pl.pallas_call(
        pack_kernel,
        out_shape=(S((planes, fields, rows, cols), f32), payload, payload),
        in_specs=[ANY, VMEM, VMEM],
        out_specs=(VMEM, VMEM, VMEM),
        scratch_shapes=[pltpu.VMEM((fields, members, rows, cols), f32), pltpu.SemaphoreType.DMA((fields,))],
        compiler_params=PARAMS,
        name="pack",
    )(ensemble, depth_class, idx)

    inner = [(i, i ^ 1) for i in range(ncol)]
    outer = [(i, (i + 1) % ncol if i % 2 else (i - 1) % ncol) for i in range(ncol)]

    def exchange(a, b):
        rb = lax.ppermute(b, "col", outer)
        ra = lax.ppermute(a, "col", inner)
        return ra, rb

    ra, rb = exchange(pa, pb)
    block = 4
    raw = pl.pallas_call(
        forecast_kernel,
        out_shape=S(ensemble.shape, f32),
        grid=(members // block,),
        in_specs=[
            pl.BlockSpec((block, fields, rows, cols), lambda m: (m, 0, 0, 0)),
            pl.BlockSpec((rows, cols), lambda m: (0, 0)),
        ],
        out_specs=pl.BlockSpec((block, fields, rows, cols), lambda m: (m, 0, 0, 0)),
        compiler_params=PARAMS,
        name="forecast",
    )(ensemble, depth_class)

    edges, loss = pl.pallas_call(
        edge_kernel,
        out_shape=(S((planes, fields, rows, cols), f32), S((members, nobs), f32)),
        in_specs=[VMEM, VMEM, VMEM, VMEM, ANY, VMEM, VMEM],
        out_specs=(VMEM, VMEM),
        scratch_shapes=[
            pltpu.VMEM((members, rows, cols), f32),
            pltpu.VMEM((2, fields + 1, rows, cols), f32),
            pltpu.VMEM((per * rows, 2 * cols), bf16),
            pltpu.VMEM((per * rows, cols), bf16),
            pltpu.VMEM((per * rows, nobs), f32),
            pltpu.SemaphoreType.DMA,
        ],
        compiler_params=PARAMS,
        name="edges",
    )(ra, rb, packed, depth_class, raw, idx, obs)

    la, lb = exchange(loss, loss)
    wide = rows // 16 * cols
    own = pl.pallas_call(
        functools.partial(own_kernel, radius=radius, cols=cols, rows=rows),
        out_shape=S((16 * members, wide), f32),
        in_specs=[VMEM, VMEM],
        out_specs=VMEM,
        scratch_shapes=[pltpu.VMEM((3, 16 * members, nobs), bf16), pltpu.VMEM((wide, nobs), bf16)],
        compiler_params=PARAMS,
        name="own",
    )(loss, idx)

    part = S((fields + 2, rows // ndom, cols), f32)
    sums = pl.pallas_call(
        functools.partial(weigh_kernel, radius=radius, parts=ndom),
        out_shape=(part,) * ndom,
        in_specs=[VMEM, VMEM, VMEM, VMEM, VMEM, ANY, VMEM, VMEM],
        out_specs=(VMEM,) * ndom,
        scratch_shapes=[
            pltpu.VMEM((3, 16 * members, 2 * nobs), bf16),
            pltpu.VMEM((wide, 2 * nobs), bf16),
            pltpu.VMEM((16 * members, wide), f32),
            pltpu.VMEM((members, rows, cols), f32),
            pltpu.VMEM((fields + 2, rows, cols), f32),
            pltpu.VMEM((members, fields, rows, cols), f32),
            pltpu.SemaphoreType.DMA,
        ],
        compiler_params=PARAMS,
        name="weigh",
    )(own, la, lb, ra, rb, raw, edges, annealing_exponents)

    parts = [sums[0]] + [swap(sums[k], k, ndom) for k in range(1, ndom)]
    mine = pl.pallas_call(
        join_kernel,
        out_shape=S((fields, rows // ndom, cols), f32),
        in_specs=[VMEM] * ndom,
        out_specs=VMEM,
        compiler_params=PARAMS,
        name="join",
    )(*parts)
    blocks = [mine] + [swap(mine, k, ndom) for k in range(1, ndom)]
    return pl.pallas_call(
        place_kernel,
        out_shape=S((fields, rows, cols), f32),
        in_specs=[VMEM] * ndom,
        out_specs=VMEM,
        compiler_params=PARAMS,
        name="place",
    )(*blocks)


def solution(mesh):
    in_specs = (P("dom", None, None, "col"), P(None, "col"), P("col"), P("col"), P(None, "col"))
    out_specs = P(None, None, "col")
    return jax.shard_map(
        on_device, mesh=mesh, in_specs=in_specs, out_specs=out_specs, check_vma=False
    )
```

time: 209 us -> 80.8 us (0.39)
  other arithmetic: 72.4 us -> 0 us
  local copies, waits for them, and re-layouts: 67.4 us -> 2.7 us
  Pallas kernels: 0 us -> 55.3 us
  blocking collectives: 30.6 us -> 0 us
  matrix products: 7.46 us -> 0 us
  waiting for transfers between devices: 14.3 us -> 9.78 us
  starting transfers between devices: 15.3 us -> 12.4 us
    pallas_call x0 -> x7, Pallas kernels: none -> 55.3 us  [the longest x1 14.3 us: on_device(): pl.pallas_call(forecast_kernel, out_shape=S(ensemble.shape, f32), grid=(m...]
    all_gather x3 -> x0, blocking collectives: 30.6 us -> none  [joined(): gathered = jax.tree.map(lambda a: lax.all_gather(a, axis), part)]
    slice x13 -> x0, local copies, waits for them, and re-layouts: 25.1 us -> none  [the longest x6 16.9 us: diff_rows(): return 0.5 * (padded[..., 2:, :] - padded[..., :-2, :])]
    scatter-add x1 -> x0, other arithmetic: 23.2 us -> none  [on_device(): loglik = jnp.zeros((ensemble_solutions, number_of_meridional_lines * numb...]
    sub x4 -> x0, other arithmetic: 19.7 us -> none  [the longest x2 17.3 us: integrate_model_ahead(): tracers[..., 2:-2]]
    broadcast_in_dim x3 -> x0, local copies, waits for them, and re-layouts: 10.8 us -> none  [the longest x2 8.13 us: integrate_model_ahead(): merid_new[..., None, :, 1:-1]]
    unnamed x39 -> x20, local copies, waits for them, and re-layouts: 12.4 us -> 2.7 us
    reduce_sum x2 -> x0, other arithmetic: 8.32 us -> none  [the longest x1 6.93 us: on_device(): jnp.sum(sample_importance[:, None] * prior_solution, axis=0)]
  transfers between devices with their start and end apart: 8 -> 10, of which waited for: 3 -> 7; matrix products, arithmetic and copies ran while one was open for 8% -> 0% of each run, Pallas kernels for 0% -> 23%
where the time goes in v1:
time: 80.8 us; the launch traced here: 80.3 us
  Pallas kernels  55.3 us (68%)
  starting transfers between devices  12.4 us (15%)
  waiting for transfers between devices  9.78 us (12%)
  local copies, waits for them, and re-layouts  2.7 us (3%)
    pallas_call x1, Pallas kernels, on_device(): pl.pallas_call(forecast_kernel, out_shape=S(ensemble.shape, f32), grid=(m...  14.3 us
    pallas_call x1, Pallas kernels, on_device(): pl.pallas_call(pack_kernel, out_shape=(S((planes, fields, rows, cols), f3...  12.3 us
    pallas_call x1, Pallas kernels, on_device(): pl.pallas_call(functools.partial(weigh_kernel, radius=radius, parts=ndom)...  11.1 us
    pallas_call x1, Pallas kernels, on_device(): pl.pallas_call(edge_kernel, out_shape=(S((planes, fields, rows, cols), f3...  10 us
    ppermute x6, waiting for transfers between devices, swap(): lax.ppermute(x, 'dom', [(i, i ^ k if count & count - 1 == 0 else (i + k)...  8.05 us
    ppermute x6, starting transfers between devices, swap(): lax.ppermute(x, 'dom', [(i, i ^ k if count & count - 1 == 0 else (i + k)...  7.04 us
    ppermute x2, starting transfers between devices, exchange(): rb = lax.ppermute(b, 'col', outer)  4.77 us
    pallas_call x1, Pallas kernels, on_device(): pl.pallas_call(functools.partial(own_kernel, radius=radius, cols=cols, ro...  4.23 us
  transfers between devices with their start and end apart: 10, of which 7 were waited for; matrix products, arithmetic and copies ran while one was open for 0% of the time, Pallas kernels for 23%

profile of v1, /device:TPU:0, one launch (start us, length us, event | category | flops | bytes accessed | tf_op | source)
XLA Modules:
  0.0 80.3 jit_solution(5550059406529113119)
XLA Ops:
  0.0 12.3 %pack.1 = (f32[4,5,96,128]{3,2,1,0:T(8,128)}, f32[392,128]{1,0:T(8,128)}, f32[392,128]{1,0:T(8,128)}) custom-call(f32[32,5,96,128]{3,2,1,0:T(8,128)} %x_ref.1, s32[96,128]{1,0:T(8,128)} %cls_ref.5, s32[6,128]{1,0:T(8,128)} %bitcast.2), custom_call_target="tpu_custom_call" | custom-call | tf_op jit(solution)/shard_map/pack/pallas_call | solution.py:385
  12.3 0.6 collective-permute-start
  12.9 4.7 %collective-permute-start.1 = (f32[392,128]{1,0:T(8,128)}, f32[392,128]{1,0:T(8,128)S(1)}, u32[]{:S(2)}, u32[]{:S(2)}) collective-permute-start(f32[392,128]{1,0:T(8,128)} %get-tuple-element.15), channel_id=1, source_target_pairs={{0,7},{1,2},{2,1},{3,4},{4,3},{5,6},{6,5},{7,0},{8,15},{9,10},{10,... | collective-permute-start | bytes 602120 | tf_op jit(solution)/shard_map/ppermute | solution.py:399
  17.6 14.3 %forecast.1.x_hbm = f32[32,5,96,128]{3,2,1,0:T(8,128)} custom-call(f32[32,5,96,128]{3,2,1,0:T(8,128)} %x_ref.1, s32[96,128]{1,0:T(8,128)} %cls_ref.5), custom_call_target="tpu_custom_call" | custom-call | tf_op jit(solution)/shard_map/forecast/pallas_call | solution.py:405
  31.9 0.0 collective-permute-done.ra_ref
  31.9 0.0 copy-start
  31.9 0.0 collective-permute-done.1.rb_ref
  31.9 0.0 copy-start.1
  31.9 0.7 copy-done
  32.6 0.1 copy-done.1
  32.7 10.0 %edges.1 = (f32[4,5,96,128]{3,2,1,0:T(8,128)}, f32[32,768]{1,0:T(8,128)}) custom-call(f32[392,128]{1,0:T(8,128)} %copy-done, f32[392,128]{1,0:T(8,128)} %copy-done.1, f32[4,5,96,128]{3,2,1,0:T(8,128)} %get-tuple-element.16.g_ref, s32[96,128]{1,0:T(8,128)} %cls_ref.5, f32[32,5,96,128]{3,2,1,0:T(8,128)} %forecast.1.x_hbm, s32[6,128]{1,0:T(8,128)} %bitcast.3, ...), custom_call_target="tpu_custom_call" | custom-call | tf_op jit(solution)/shard_map/edges/pallas_call | solution.py:418
  42.7 0.1 collective-permute-start.3
  42.8 0.1 collective-permute-start.2
  42.8 4.2 %own.1.own_ref = f32[512,768]{1,0:T(8,128)} custom-call(f32[32,768]{1,0:T(8,128)} %get-tuple-element.17.loss_ref, s32[6,128]{1,0:T(8,128)} %bitcast.4), custom_call_target="tpu_custom_call" | custom-call | tf_op jit(solution)/shard_map/own/pallas_call | solution.py:437
  47.1 1.7 %collective-permute-done.3.lb_ref = f32[32,768]{1,0:T(8,128)S(1)} collective-permute-done((f32[32,768]{1,0:T(8,128)}, f32[32,768]{1,0:T(8,128)S(1)}, u32[]{:S(2)}, u32[]{:S(2)}) %collective-permute-start.3) | collective-permute-done | bytes 98336 | tf_op jit(solution)/shard_map/ppermute | solution.py:399
  48.8 0.0 copy-start.2
  48.8 0.0 collective-permute-done.2.la_ref
  48.8 0.0 copy-start.3
  48.8 0.6 copy-done.2
  49.4 0.1 copy-done.3
  49.5 11.1 %weigh.1 = (f32[7,24,128]{2,1,0:T(8,128)}, f32[7,24,128]{2,1,0:T(8,128)}, f32[7,24,128]{2,1,0:T(8,128)}, f32[7,24,128]{2,1,0:T(8,128)}) custom-call(f32[512,768]{1,0:T(8,128)} %own.1.own_ref, f32[32,768]{1,0:T(8,128)} %copy-done.3, f32[32,768]{1,0:T(8,128)} %copy-done.2, f32[392,128]{1,0:T(8,128)} %copy-done, f32[392,128]{1,0:T(8,128)} %copy-done.1, ...), custom_call_target="tpu_custom_call" | custom-call | tf_op jit(solution)/shard_map/weigh/pallas_call | solution.py:448
  60.6 1.6 %collective-permute-start.4 = (f32[7,24,128]{2,1,0:T(8,128)}, f32[7,24,128]{2,1,0:T(8,128)S(1)}, u32[]{:S(2)}, u32[]{:S(2)}) collective-permute-start(f32[7,24,128]{2,1,0:T(8,128)} %get-tuple-element.20), channel_id=1, source_target_pairs={{0,8},{8,0},{16,24},{24,16},{1,9},{9,1},{17,25},{25,17},{2,10},{10... | collective-permute-start | bytes 258056 | tf_op jit(solution)/shard_map/ppermute | solution.py:344
  62.1 1.5 %collective-permute-start.5 = (f32[7,24,128]{2,1,0:T(8,128)}, f32[7,24,128]{2,1,0:T(8,128)S(1)}, u32[]{:S(2)}, u32[]{:S(2)}) collective-permute-start(f32[7,24,128]{2,1,0:T(8,128)} %get-tuple-element.21), channel_id=1, source_target_pairs={{0,16},{8,24},{16,0},{24,8},{1,17},{9,25},{17,1},{25,9},{2,18},{10... | collective-permute-start | bytes 258056 | tf_op jit(solution)/shard_map/ppermute | solution.py:344
  63.7 0.5 collective-permute-start.6
  64.1 1.9 %collective-permute-done.4.refs_1_ = f32[7,24,128]{2,1,0:T(8,128)S(1)} collective-permute-done((f32[7,24,128]{2,1,0:T(8,128)}, f32[7,24,128]{2,1,0:T(8,128)S(1)}, u32[]{:S(2)}, u32[]{:S(2)}) %collective-permute-start.4) | collective-permute-done | bytes 86048 | tf_op jit(solution)/shard_map/ppermute | solution.py:344
  66.1 0.0 copy-start.4
  66.1 1.5 %collective-permute-done.5.refs_2_ = f32[7,24,128]{2,1,0:T(8,128)S(1)} collective-permute-done((f32[7,24,128]{2,1,0:T(8,128)}, f32[7,24,128]{2,1,0:T(8,128)S(1)}, u32[]{:S(2)}, u32[]{:S(2)}) %collective-permute-start.5) | collective-permute-done | bytes 86048 | tf_op jit(solution)/shard_map/ppermute | solution.py:344
  67.6 0.0 copy-start.5
  67.6 1.7 %collective-permute-done.6.refs_3_ = f32[7,24,128]{2,1,0:T(8,128)S(1)} collective-permute-done((f32[7,24,128]{2,1,0:T(8,128)}, f32[7,24,128]{2,1,0:T(8,128)S(1)}, u32[]{:S(2)}, u32[]{:S(2)}) %collective-permute-start.6) | collective-permute-done | bytes 86048 | tf_op jit(solution)/shard_map/ppermute | solution.py:344
  69.2 0.0 copy-start.6
  69.2 0.0 copy-done.4
  69.3 0.0 copy-done.5
  69.3 0.6 copy-done.6
  69.9 1.7 %join.1.refs_0_ = f32[5,24,128]{2,1,0:T(8,128)} custom-call(f32[7,24,128]{2,1,0:T(8,128)} %get-tuple-element.19.refs_0_, f32[7,24,128]{2,1,0:T(8,128)} %copy-done.4, f32[7,24,128]{2,1,0:T(8,128)} %copy-done.5, f32[7,24,128]{2,1,0:T(8,128)} %copy-done.6), custom_call_target="tpu_custom_call" | custom-call | tf_op jit(solution)/shard_map/join/pallas_call | solution.py:467
  71.6 0.5 collective-permute-start.9
  72.0 1.5 %collective-permute-start.8 = (f32[5,24,128]{2,1,0:T(8,128)}, f32[5,24,128]{2,1,0:T(8,128)S(1)}, u32[]{:S(2)}, u32[]{:S(2)}) collective-permute-start(f32[5,24,128]{2,1,0:T(8,128)} %join.1.refs_0_), channel_id=1, source_target_pairs={{0,16},{8,24},{16,0},{24,8},{1,17},{9,25},{17,1},{25,9},{2,18},{10... | collective-permute-start | bytes 184328 | tf_op jit(solution)/shard_map/ppermute | solution.py:344
  73.6 1.5 %collective-permute-start.7 = (f32[5,24,128]{2,1,0:T(8,128)}, f32[5,24,128]{2,1,0:T(8,128)S(1)}, u32[]{:S(2)}, u32[]{:S(2)}) collective-permute-start(f32[5,24,128]{2,1,0:T(8,128)} %join.1.refs_0_), channel_id=1, source_target_pairs={{0,8},{8,0},{16,24},{24,16},{1,9},{9,1},{17,25},{25,17},{2,10},{10... | collective-permute-start | bytes 184328 | tf_op jit(solution)/shard_map/ppermute | solution.py:344
  75.0 1.9 %collective-permute-done.9.refs_3_ = f32[5,24,128]{2,1,0:T(8,128)S(1)} collective-permute-done((f32[5,24,128]{2,1,0:T(8,128)}, f32[5,24,128]{2,1,0:T(8,128)S(1)}, u32[]{:S(2)}, u32[]{:S(2)}) %collective-permute-start.9) | collective-permute-done | bytes 61472 | tf_op jit(solution)/shard_map/ppermute | solution.py:344
  77.0 0.0 copy-start.7
  77.0 0.1 collective-permute-done.8.refs_2_
  77.1 0.0 copy-start.8
  77.1 0.9 %collective-permute-done.7.refs_1_ = f32[5,24,128]{2,1,0:T(8,128)S(1)} collective-permute-done((f32[5,24,128]{2,1,0:T(8,128)}, f32[5,24,128]{2,1,0:T(8,128)S(1)}, u32[]{:S(2)}, u32[]{:S(2)}) %collective-permute-start.7) | collective-permute-done | bytes 61472 | tf_op jit(solution)/shard_map/ppermute | solution.py:344
  78.0 0.0 copy-done.7
  78.0 0.0 copy-done.8
  78.0 0.0 copy-start.9
  78.0 0.6 copy-done.9
  78.6 1.6 %place.1 = f32[5,96,128]{2,1,0:T(8,128)} custom-call(f32[5,24,128]{2,1,0:T(8,128)} %join.1.refs_0_, f32[5,24,128]{2,1,0:T(8,128)} %copy-done.9, f32[5,24,128]{2,1,0:T(8,128)} %copy-done.8, f32[5,24,128]{2,1,0:T(8,128)} %copy-done.7), custom_call_target="tpu_custom_call" | custom-call | tf_op jit(solution)/shard_map/place/pallas_call | solution.py:476
Async XLA Ops:
  12.3 19.6 %collective-permute-start = (f32[392,128]{1,0:T(8,128)}, f32[392,128]{1,0:T(8,128)S(1)}, u32[]{:S(2)}, u32[]{:S(2)}) collective-permute-start(f32[392,128]{1,0:T(8,128)} %get-tuple-element.14), channel_id=1, source_target_pairs={{0,1},{1,0},{2,3},{3,2},{4,5},{5,4},{6,7},{7,6},{8,9},{9,8},{10,11... | collective-permute-start | bytes 602120 | tf_op jit(solution)/shard_map/ppermute | solution.py:400
  12.9 19.0 %collective-permute-start.1 = (f32[392,128]{1,0:T(8,128)}, f32[392,128]{1,0:T(8,128)S(1)}, u32[]{:S(2)}, u32[]{:S(2)}) collective-permute-start(f32[392,128]{1,0:T(8,128)} %get-tuple-element.15), channel_id=1, source_target_pairs={{0,7},{1,2},{2,1},{3,4},{4,3},{5,6},{6,5},{7,0},{8,15},{9,10},{10,... | collective-permute-start | bytes 602120 | tf_op jit(solution)/shard_map/ppermute | solution.py:399
  31.9 0.7 copy-start
  31.9 0.8 copy-start.1
  42.7 6.1 %collective-permute-start.3 = (f32[32,768]{1,0:T(8,128)}, f32[32,768]{1,0:T(8,128)S(1)}, u32[]{:S(2)}, u32[]{:S(2)}) collective-permute-start(f32[32,768]{1,0:T(8,128)} %get-tuple-element.17.loss_ref), channel_id=1, source_target_pairs={{0,7},{1,2},{2,1},{3,4},{4,3},{5,6},{6,5},{7,0},{8,15},{9,10},{10,... | collective-permute-start | bytes 294920 | tf_op jit(solution)/shard_map/ppermute | solution.py:399
  42.8 6.0 %collective-permute-start.2 = (f32[32,768]{1,0:T(8,128)}, f32[32,768]{1,0:T(8,128)S(1)}, u32[]{:S(2)}, u32[]{:S(2)}) collective-permute-start(f32[32,768]{1,0:T(8,128)} %get-tuple-element.17.loss_ref), channel_id=1, source_target_pairs={{0,1},{1,0},{2,3},{3,2},{4,5},{5,4},{6,7},{7,6},{8,9},{9,8},{10,11... | collective-permute-start | bytes 294920 | tf_op jit(solution)/shard_map/ppermute | solution.py:400
  48.8 0.6 copy-start.2
  48.8 0.7 copy-start.3
  60.6 5.5 %collective-permute-start.4 = (f32[7,24,128]{2,1,0:T(8,128)}, f32[7,24,128]{2,1,0:T(8,128)S(1)}, u32[]{:S(2)}, u32[]{:S(2)}) collective-permute-start(f32[7,24,128]{2,1,0:T(8,128)} %get-tuple-element.20), channel_id=1, source_target_pairs={{0,8},{8,0},{16,24},{24,16},{1,9},{9,1},{17,25},{25,17},{2,10},{10... | collective-permute-start | bytes 258056 | tf_op jit(solution)/shard_map/ppermute | solution.py:344
  62.1 5.4 %collective-permute-start.5 = (f32[7,24,128]{2,1,0:T(8,128)}, f32[7,24,128]{2,1,0:T(8,128)S(1)}, u32[]{:S(2)}, u32[]{:S(2)}) collective-permute-start(f32[7,24,128]{2,1,0:T(8,128)} %get-tuple-element.21), channel_id=1, source_target_pairs={{0,16},{8,24},{16,0},{24,8},{1,17},{9,25},{17,1},{25,9},{2,18},{10... | collective-permute-start | bytes 258056 | tf_op jit(solution)/shard_map/ppermute | solution.py:344
  63.7 5.6 %collective-permute-start.6 = (f32[7,24,128]{2,1,0:T(8,128)}, f32[7,24,128]{2,1,0:T(8,128)S(1)}, u32[]{:S(2)}, u32[]{:S(2)}) collective-permute-start(f32[7,24,128]{2,1,0:T(8,128)} %get-tuple-element.22), channel_id=1, source_target_pairs={{0,24},{8,16},{16,8},{24,0},{1,25},{9,17},{17,9},{25,1},{2,26},{10... | collective-permute-start | bytes 258056 | tf_op jit(solution)/shard_map/ppermute | solution.py:344
  66.1 3.2 %copy-start.4 = (f32[7,24,128]{2,1,0:T(8,128)}, f32[7,24,128]{2,1,0:T(8,128)S(1)}, u32[]{:S(2)}) copy-start(f32[7,24,128]{2,1,0:T(8,128)S(1)} %collective-permute-done.4.refs_1_) | copy-start | bytes 258052
  67.6 1.7 %copy-start.5 = (f32[7,24,128]{2,1,0:T(8,128)}, f32[7,24,128]{2,1,0:T(8,128)S(1)}, u32[]{:S(2)}) copy-start(f32[7,24,128]{2,1,0:T(8,128)S(1)} %collective-permute-done.5.refs_2_) | copy-start | bytes 258052
  69.2 0.6 copy-start.6
  71.6 5.4 %collective-permute-start.9 = (f32[5,24,128]{2,1,0:T(8,128)}, f32[5,24,128]{2,1,0:T(8,128)S(1)}, u32[]{:S(2)}, u32[]{:S(2)}) collective-permute-start(f32[5,24,128]{2,1,0:T(8,128)} %join.1.refs_0_), channel_id=1, source_target_pairs={{0,24},{8,16},{16,8},{24,0},{1,25},{9,17},{17,9},{25,1},{2,26},{10... | collective-permute-start | bytes 184328 | tf_op jit(solution)/shard_map/ppermute | solution.py:344
  72.0 5.1 %collective-permute-start.8 = (f32[5,24,128]{2,1,0:T(8,128)}, f32[5,24,128]{2,1,0:T(8,128)S(1)}, u32[]{:S(2)}, u32[]{:S(2)}) collective-permute-start(f32[5,24,128]{2,1,0:T(8,128)} %join.1.refs_0_), channel_id=1, source_target_pairs={{0,16},{8,24},{16,0},{24,8},{1,17},{9,25},{17,1},{25,9},{2,18},{10... | collective-permute-start | bytes 184328 | tf_op jit(solution)/shard_map/ppermute | solution.py:344
  73.6 4.4 %collective-permute-start.7 = (f32[5,24,128]{2,1,0:T(8,128)}, f32[5,24,128]{2,1,0:T(8,128)S(1)}, u32[]{:S(2)}, u32[]{:S(2)}) collective-permute-start(f32[5,24,128]{2,1,0:T(8,128)} %join.1.refs_0_), channel_id=1, source_target_pairs={{0,8},{8,0},{16,24},{24,16},{1,9},{9,1},{17,25},{25,17},{2,10},{10... | collective-permute-start | bytes 184328 | tf_op jit(solution)/shard_map/ppermute | solution.py:344
  77.0 1.0 %copy-start.7 = (f32[5,24,128]{2,1,0:T(8,128)}, f32[5,24,128]{2,1,0:T(8,128)S(1)}, u32[]{:S(2)}) copy-start(f32[5,24,128]{2,1,0:T(8,128)S(1)} %collective-permute-done.9.refs_3_) | copy-start | bytes 184324
  77.1 0.9 %copy-start.8 = (f32[5,24,128]{2,1,0:T(8,128)}, f32[5,24,128]{2,1,0:T(8,128)S(1)}, u32[]{:S(2)}) copy-start(f32[5,24,128]{2,1,0:T(8,128)S(1)} %collective-permute-done.8.refs_2_) | copy-start | bytes 184324
  78.0 0.6 copy-start.9

commit v2 on v1

--- a/solution.py
+++ b/solution.py
@@ -12,12 +12,17 @@
 CORIOLIS = 0.2
 GROUP = 16
 EDGE = 4
+ZEROS = 8
+BANDS = 4
 HALF = 8
-VMEM = pl.BlockSpec(memory_space=pltpu.VMEM)
-ANY = pl.BlockSpec(memory_space=pl.ANY)
-PARAMS = pltpu.CompilerParams(vmem_limit_bytes=56 * 1024 * 1024)
 f32 = jnp.float32
 bf16 = jnp.bfloat16
+VMEM = pl.BlockSpec(memory_space=pltpu.VMEM)
+HBM = pl.BlockSpec(memory_space=pltpu.HBM)
+
+
+def params(mib):
+    return pltpu.CompilerParams(vmem_limit_bytes=mib * 1024 * 1024)
 
 
 def depth_of(cls):
@@ -32,29 +37,45 @@
     return pltpu.roll(x, shift % x.shape[-1] if isinstance(shift, int) else shift, x.ndim - 1)
 
 
-def step(fields, depth, first, last):
+def shift_table(cols):
+    k = lax.broadcasted_iota(jnp.int32, (2 * cols, cols), 0) & (cols - 1)
+    c = lax.broadcasted_iota(jnp.int32, (2 * cols, cols), 1)
+    return (jnp.where(k == c + 1, 1.0, 0.0) - jnp.where(k == c - 1, 1.0, 0.0)).astype(bf16)
+
+
+def step(fields, depth, pad, slot, table):
     h, u, v, a, b = fields
     rows = h.shape[0]
 
     def cols(q):
         return roll_lanes(q, -1) - roll_lanes(q, 1)
 
-    def rws(q):
-        return jnp.where(last, 0.0, pltpu.roll(q, rows - 1, 0)) - jnp.where(first, 0.0, pltpu.roll(q, 1, 0))
-
+    def rws(q, n):
+        pad[slot + n, ZEROS : ZEROS + rows, :] = q
+        return pad[slot + n, ZEROS + 1 : ZEROS + 1 + rows, :] - pad[slot + n, ZEROS - 1 : ZEROS - 1 + rows, :]
+
+    both = jnp.concatenate([a, b], axis=0)
+    hi = both.astype(bf16)
+    mid = (both - hi.astype(f32)).astype(bf16)
+    slopes = jnp.dot(jnp.concatenate([hi, mid], axis=1), table[...], preferred_element_type=f32)
     half = 0.5 * TIME_STEP
     un = u - half * cols(h) + TIME_STEP * CORIOLIS * v
-    vn = v - half * rws(h) - TIME_STEP * CORIOLIS * u
-    hn = h - half * (cols(depth * un) + rws(depth * vn))
-    an = a - half * (un * cols(a) + vn * rws(a))
-    bn = b - half * (un * cols(b) + vn * rws(b))
+    vn = v - half * rws(h, 0) - TIME_STEP * CORIOLIS * u
+    hn = h - half * (cols(depth * un) + rws(depth * vn, 1))
+    an = a - half * (un * slopes[:rows] + vn * rws(a, 2))
+    bn = b - half * (un * slopes[rows:] + vn * rws(b, 3))
     return hn, un, vn, an, bn
 
 
-def two_steps(fields, depth):
-    rid = lax.broadcasted_iota(jnp.int32, depth.shape, 0)
-    first, last = rid == 0, rid == depth.shape[0] - 1
-    return step(step(fields, depth, first, last), depth, first, last)
+def prepare(pad, table):
+    for n in range(pad.shape[0]):
+        pad[n, :ZEROS, :] = jnp.zeros((ZEROS, pad.shape[2]), f32)
+        pad[n, pad.shape[1] - ZEROS :, :] = jnp.zeros((ZEROS, pad.shape[2]), f32)
+    table[...] = shift_table(table.shape[1])
+
+
+def two_steps(fields, depth, pad, table, slot=0):
+    return step(step(fields, depth, pad, slot, table), depth, pad, slot + 4, table)
 
 
 def pack_kernel(x_hbm, cls_ref, idx_ref, g_ref, pa_ref, pb_ref, buf, sem):
@@ -105,7 +126,7 @@
             put(f, t, right, left)
             return carry
 
-        lax.fori_loop(0, rows // 8, body, 0)
+        lax.fori_loop(0, rows // 8, body, 0, unroll=4)
     copies[3].wait()
     copies[4].wait()
 
@@ -115,23 +136,24 @@
         put(3, t, jnp.where(jj >= 2, ra, roll_lanes(rb, -2)), jnp.where(jj < 2, la, roll_lanes(lb, 2)))
         return carry
 
-    lax.fori_loop(0, rows // 8, tracers, 0)
+    lax.fori_loop(0, rows // 8, tracers, 0, unroll=2)
     n = idx_ref.shape[0]
     for ref in (pa_ref, pb_ref):
         ref[4 * rows : 4 * rows + 8, :] = jnp.zeros((8, cols), f32)
         ref[4 * rows : 4 * rows + n, :] = idx_ref[...].astype(f32)
 
 
-def forecast_kernel(x_ref, cls_ref, o_ref):
+def forecast_kernel(x_ref, cls_ref, o_ref, pad, table):
     depth = depth_of(cls_ref[...])
+    pl.when(pl.program_id(0) == 0)(lambda: prepare(pad, table))
 
     def body(m, carry):
-        out = two_steps([x_ref[m, f] for f in range(5)], depth)
+        out = two_steps([x_ref[m, f] for f in range(5)], depth, pad, table)
         for f in range(5):
             o_ref[m, f] = out[f]
         return carry
 
-    lax.fori_loop(0, x_ref.shape[0], body, 0)
+    lax.fori_loop(0, x_ref.shape[0], body, 0, unroll=4)
 
 
 def pieces_of(x):
@@ -146,13 +168,11 @@
     return jnp.concatenate([x[i : i + 1, :] for i in range(x.shape[0])], axis=1)
 
 
-def edge_kernel(ra_ref, rb_ref, g_ref, cls_ref, x_hbm, idx_ref, obs_ref, z_ref, loss_ref, hbuf, xs, lhs, low, prod, sem):
-    members, _, rows, cols = x_hbm.shape
+def edge_kernel(ra_ref, rb_ref, g_ref, cls_ref, x_ref, idx_ref, obs_ref, z_ref, loss_ref, xs, pad, table, lhs, low, prod):
+    members, _, rows, cols = x_ref.shape
     per = cols // GROUP
     planes = members // per
     even = lax.rem(lax.axis_index("col"), 2) == 0
-    copy = pltpu.make_async_copy(x_hbm.at[:, 0], hbuf, sem)
-    copy.start()
     lane = lanes_of((rows, cols))
     j = lane % GROUP
     grp = lane // GROUP
@@ -191,13 +211,14 @@
             hr = pltpu.roll(xs[1, f], lax.rem(cols + HALF - EDGE * q, cols), 1)
             left.append(jnp.where(j < EDGE, hl, roll_lanes(g, -EDGE)))
             right.append(jnp.where(j >= HALF, hr, g))
-        left = two_steps(left, xs[0, 5])
-        right = two_steps(right, xs[1, 5])
+        left = two_steps(left, xs[0, 5], pad, table)
+        right = two_steps(right, xs[1, 5], pad, table, 8)
         inner = (j >= EDGE) & (j < 2 * EDGE)
         for f in range(5):
             z_ref[q, f] = jnp.where(inner, right[f], roll_lanes(left[f], EDGE))
         return carry
 
+    prepare(pad, table)
     lax.fori_loop(0, planes, strips, 0)
 
     idx = row_vector(idx_ref[...])
@@ -208,12 +229,11 @@
     pick2 = jnp.concatenate([pick, pick], axis=0)
     isrow = lax.broadcasted_iota(jnp.int32, (rows, nobs), 0) == row
     border = (lane < EDGE) | (lane >= cols - EDGE)
-    copy.wait()
 
     def gather(q, carry):
         for i in range(per):
             at = slice(i * rows, (i + 1) * rows)
-            h = jnp.where(border, roll_lanes(z_ref[q, 0], cols - HALF - GROUP * i), hbuf[q * per + i])
+            h = jnp.where(border, roll_lanes(z_ref[q, 0], cols - HALF - GROUP * i), x_ref[q * per + i, 0])
             hi, mid, lo = pieces_of(h)
             lhs[at, :cols] = hi
             lhs[at, cols:] = mid
@@ -232,81 +252,102 @@
     lax.fori_loop(0, planes, gather, 0)
 
 
-def spread(losses, indices, offsets, radius, cols, rows, lhs, rhs):
-    members = losses[0].shape[0]
-    start = 0
-    for loss, idx, offset in zip(losses, indices, offsets):
-        n = idx.shape[1]
-        at = slice(start, start + n)
-        start += n
-        row, col = lax.shift_right_logical(idx, cols.bit_length() - 1), idx & (cols - 1)
-        dist = jnp.abs(lax.broadcasted_iota(jnp.int32, (cols, n), 0) - (col + offset))
-        table = jnp.maximum(0, radius + 1 - dist).astype(f32)
-        block = lax.shift_right_logical(row, 4)
-        for b in range(rows // 16):
-            rhs[b * cols : (b + 1) * cols, at] = jnp.where(block == b, table, 0.0).astype(bf16)
-        isrow = lax.broadcasted_iota(jnp.int32, (16, n), 0) == (row & 15)
-        parts = [p.astype(f32) for p in pieces_of(loss)]
-        for m in range(members):
-            for p in range(3):
-                lhs[p, 16 * m : 16 * m + 16, at] = jnp.where(isrow, parts[p][m : m + 1, :], 0.0).astype(bf16)
+def spread(loss, idx, offset, first, width, order, radius, cols, rows, lhs, rhs):
+    members, n = loss.shape
+    band = rows // BANDS
+    col = idx & (cols - 1)
+    row = lax.shift_right_logical(idx, cols.bit_length() - 1)
+    dist = jnp.abs(lax.broadcasted_iota(jnp.int32, (width, n), 0) + (first - offset) - col)
+    table = jnp.maximum(0, radius + 1 - dist).astype(f32)
+    block = sum(jnp.where(row >= band * b, 1, 0) for b in range(1, BANDS))
+    for pos, b in enumerate(order):
+        rhs[pos * width : (pos + 1) * width, :] = jnp.where(block == b, table, 0.0).astype(bf16)
+    isrow = lax.broadcasted_iota(jnp.int32, (band, n), 0) == row - band * block
+    for p, part in enumerate(pieces_of(loss)):
+        part = part.astype(f32)
+        for m in range(0, members, 2):
+            pair = [jnp.where(isrow, part[m + i : m + i + 1, :], 0.0) for i in range(2)]
+            lhs[p, band * m : band * (m + 2), :] = jnp.concatenate(pair, axis=0).astype(bf16)
     dims = (((1,), (1,)), ((), ()))
     return sum(lax.dot_general(lhs[p], rhs[...], dims, preferred_element_type=f32) for p in range(3))
 
 
 def own_kernel(loss_ref, idx_ref, o_ref, lhs, rhs, *, radius, cols, rows):
-    o_ref[...] = spread([loss_ref[...]], [row_vector(idx_ref[...])], [0], radius, cols, rows, lhs, rhs)
-
-
-def weigh_kernel(own_ref, la_ref, lb_ref, ra_ref, rb_ref, x_hbm, z_ref, ann_ref, *rest, radius, parts):
+    o_ref[...] = spread(
+        loss_ref[...], row_vector(idx_ref[...]), 0, 0, cols, range(BANDS), radius, cols, rows, lhs, rhs
+    )
+
+
+def triangle(q, bufs):
+    rows = q.shape[0]
+    size = rows + 2 * ROW_REACH
+    low = 2 * ZEROS
+    bufs[0, low : low + rows, :] = q
+    start, count = ZEROS, size
+    for n, gap in enumerate((1, 3, 1, 3)):
+        if n == 3:
+            start, count = low, rows
+        y = (
+            bufs[n, start - gap : start - gap + count, :]
+            + bufs[n, start : start + count, :]
+            + bufs[n, start + gap : start + gap + count, :]
+        )
+        if n < 3:
+            bufs[n + 1, start : start + count, :] = y
+    return y
+
+
+def weigh_kernel(own_ref, la_ref, lb_ref, ra_ref, rb_ref, x_ref, z_ref, ann_ref, *rest, radius, parts):
     outs = rest[:parts]
-    lhs, rhs, acc, logw, tot, xbuf, sem = rest[parts:]
-    members, fields, rows, cols = x_hbm.shape
+    lhs, rhs, near, logw, tot, bufs = rest[parts:]
+    members, fields, rows, cols = x_ref.shape
     per = cols // GROUP
     planes = members // per
-    copy = pltpu.make_async_copy(x_hbm, xbuf, sem)
-    copy.start()
+    band = rows // BANDS
     even = lax.rem(lax.axis_index("col"), 2) == 0
     nrow = la_ref.shape[1] // cols
     at = slice(4 * rows, 4 * rows + nrow)
     ia = row_vector(ra_ref[at, :]).astype(jnp.int32)
     ib = row_vector(rb_ref[at, :]).astype(jnp.int32)
-    oa = jnp.where(even, cols, -cols)
-    acc[...] = own_ref[...] + spread(
-        [la_ref[...], lb_ref[...]], [ia, ib], [oa, -oa], radius, cols, rows, lhs, rhs
+    left = jnp.where(even, lb_ref[...], la_ref[...])
+    right = jnp.where(even, la_ref[...], lb_ref[...])
+    mid = cols // 2
+    swapped = [b ^ 1 for b in range(BANDS)]
+    near[0] = spread(
+        left, jnp.where(even, ib, ia), -cols, 0, mid, range(BANDS), radius, cols, rows, lhs.at[0], rhs.at[0]
     )
-
-    pad = jnp.zeros((ROW_REACH, cols), f32)
-    total_rows = rows + 2 * ROW_REACH
-
-    def box(q, sign):
-        def sh(x, s):
-            return pltpu.roll(x, (total_rows - s) if sign > 0 else s, 0)
-
-        out, width = q, 1
-        while 2 * width <= ROW_REACH + 1:
-            out = out + sh(out, width)
-            width *= 2
-        while width < ROW_REACH + 1:
-            out = out + sh(q, width)
-            width += 1
-        return out
+    near[1] = spread(
+        right, jnp.where(even, ia, ib), cols, mid, mid, swapped, radius, cols, rows, lhs.at[1], rhs.at[1]
+    )
+    for n in range(bufs.shape[0]):
+        for k in range(4):
+            bufs[n, k, : 2 * ZEROS, :] = jnp.zeros((2 * ZEROS, cols), f32)
+            bufs[n, k, rows + 2 * ZEROS :, :] = jnp.zeros((2 * ZEROS, cols), f32)
 
     scale = ann_ref[...] * (1.0 / ((ROW_REACH + 1) * (radius + 1)))
-
-    def smooth(m, peak):
-        at = pl.ds(pl.multiple_of(m * 16, 16), 16)
-        q = jnp.concatenate(
-            [pad] + [acc[at, b * cols : (b + 1) * cols] for b in range(rows // 16)] + [pad], axis=0
-        )
-        w = scale * box(box(q, 1), -1)[ROW_REACH : ROW_REACH + rows, :]
-        logw[m] = w
-        return jnp.maximum(peak, w)
-
-    peak = lax.fori_loop(0, members, smooth, jnp.full((rows, cols), -jnp.inf, f32))
+    lower = lanes_of((band, cols)) < mid
+
+    def smooth(g, peak):
+        for n in range(bufs.shape[0]):
+            m = g * bufs.shape[0] + n
+            at = pl.ds(pl.multiple_of(m * band, 8), band)
+            q = []
+            for b in range(0, BANDS, 2):
+                l = near[0, at, b * mid : (b + 2) * mid]
+                r = near[1, at, b * mid : (b + 2) * mid]
+                q.append(own_ref[at, b * cols : (b + 1) * cols] + jnp.where(lower, l, r))
+                q.append(
+                    own_ref[at, (b + 1) * cols : (b + 2) * cols] + roll_lanes(jnp.where(lower, r, l), mid)
+                )
+            w = scale * triangle(jnp.concatenate(q, axis=0), bufs.at[n])
+            logw[m] = w
+            peak = jnp.maximum(peak, w)
+        return peak
+
+    peak = lax.fori_loop(0, members // bufs.shape[0], smooth, jnp.full((rows, cols), -jnp.inf, f32))
     tot[fields + 1] = peak
-    copy.wait()
     lane = lanes_of((8, cols))
+    grp = lane // GROUP
     border = (lane < EDGE) | (lane >= cols - EDGE)
 
     def sums(t, carry):
@@ -314,17 +355,23 @@
         top = tot[fields + 1, at, :]
         total = jnp.zeros((8, cols), f32)
         s = [jnp.zeros((8, cols), f32)] * fields
-        for m in range(members):
-            q, i = divmod(m, per)
-            w = jnp.exp(logw[m, at, :] - top)
-            total = total + w
+        e = [jnp.zeros((8, cols), f32)] * fields
+        for q in range(planes):
+            packed = None
+            for i in range(per):
+                m = q * per + i
+                w = jnp.exp(logw[m, at, :] - top)
+                total = total + w
+                for f in range(fields):
+                    s[f] = s[f] + w * x_ref[m, f, at, :]
+                r = roll_lanes(w, GROUP * i + HALF)
+                packed = r if packed is None else jnp.where(grp == i, r, packed)
             for f in range(fields):
-                x = jnp.where(
-                    border, roll_lanes(z_ref[q, f, at, :], cols - HALF - GROUP * i), xbuf[m, f, at, :]
-                )
-                s[f] = s[f] + w * x
+                e[f] = e[f] + packed * z_ref[q, f, at, :]
         for f in range(fields):
-            tot[f, at, :] = s[f]
+            for k in (cols // 2, cols // 4, cols // 8):
+                e[f] = e[f] + roll_lanes(e[f], k)
+            tot[f, at, :] = jnp.where(border, roll_lanes(e[f], cols - HALF), s[f])
         tot[fields, at, :] = total
         return carry
 
@@ -385,10 +432,10 @@
     packed, pa, pb = pl.pallas_call(
         pack_kernel,
         out_shape=(S((planes, fields, rows, cols), f32), payload, payload),
-        in_specs=[ANY, VMEM, VMEM],
+        in_specs=[HBM, VMEM, VMEM],
         out_specs=(VMEM, VMEM, VMEM),
         scratch_shapes=[pltpu.VMEM((fields, members, rows, cols), f32), pltpu.SemaphoreType.DMA((fields,))],
-        compiler_params=PARAMS,
+        compiler_params=params(14),
         name="pack",
     )(ensemble, depth_class, idx)
 
@@ -411,36 +458,37 @@
             pl.BlockSpec((rows, cols), lambda m: (0, 0)),
         ],
         out_specs=pl.BlockSpec((block, fields, rows, cols), lambda m: (m, 0, 0, 0)),
-        compiler_params=PARAMS,
+        scratch_shapes=[pltpu.VMEM((8, rows + 2 * ZEROS, cols), f32), pltpu.VMEM((2 * cols, cols), bf16)],
+        compiler_params=params(12),
         name="forecast",
     )(ensemble, depth_class)
 
     edges, loss = pl.pallas_call(
         edge_kernel,
         out_shape=(S((planes, fields, rows, cols), f32), S((members, nobs), f32)),
-        in_specs=[VMEM, VMEM, VMEM, VMEM, ANY, VMEM, VMEM],
+        in_specs=[VMEM] * 7,
         out_specs=(VMEM, VMEM),
         scratch_shapes=[
-            pltpu.VMEM((members, rows, cols), f32),
             pltpu.VMEM((2, fields + 1, rows, cols), f32),
+            pltpu.VMEM((16, rows + 2 * ZEROS, cols), f32),
+            pltpu.VMEM((2 * cols, cols), bf16),
             pltpu.VMEM((per * rows, 2 * cols), bf16),
             pltpu.VMEM((per * rows, cols), bf16),
             pltpu.VMEM((per * rows, nobs), f32),
-            pltpu.SemaphoreType.DMA,
         ],
-        compiler_params=PARAMS,
+        compiler_params=params(18),
         name="edges",
     )(ra, rb, packed, depth_class, raw, idx, obs)
 
     la, lb = exchange(loss, loss)
-    wide = rows // 16 * cols
+    tall = members * rows // BANDS
     own = pl.pallas_call(
         functools.partial(own_kernel, radius=radius, cols=cols, rows=rows),
-        out_shape=S((16 * members, wide), f32),
+        out_shape=S((tall, BANDS * cols), f32),
         in_specs=[VMEM, VMEM],
         out_specs=VMEM,
-        scratch_shapes=[pltpu.VMEM((3, 16 * members, nobs), bf16), pltpu.VMEM((wide, nobs), bf16)],
-        compiler_params=PARAMS,
+        scratch_shapes=[pltpu.VMEM((3, tall, nobs), bf16), pltpu.VMEM((BANDS * cols, nobs), bf16)],
+        compiler_params=params(10),
         name="own",
     )(loss, idx)
 
@@ -448,18 +496,17 @@
     sums = pl.pallas_call(
         functools.partial(weigh_kernel, radius=radius, parts=ndom),
         out_shape=(part,) * ndom,
-        in_specs=[VMEM, VMEM, VMEM, VMEM, VMEM, ANY, VMEM, VMEM],
+        in_specs=[VMEM] * 8,
         out_specs=(VMEM,) * ndom,
         scratch_shapes=[
-            pltpu.VMEM((3, 16 * members, 2 * nobs), bf16),
-            pltpu.VMEM((wide, 2 * nobs), bf16),
-            pltpu.VMEM((16 * members, wide), f32),
+            pltpu.VMEM((2, 3, tall, nobs), bf16),
+            pltpu.VMEM((2, BANDS * cols // 2, nobs), bf16),
+            pltpu.VMEM((2, tall, BANDS * cols // 2), f32),
             pltpu.VMEM((members, rows, cols), f32),
             pltpu.VMEM((fields + 2, rows, cols), f32),
-            pltpu.VMEM((members, fields, rows, cols), f32),
-            pltpu.SemaphoreType.DMA,
+            pltpu.VMEM((2, 4, rows + 4 * ZEROS, cols), f32),
         ],
-        compiler_params=PARAMS,
+        compiler_params=params(30),
         name="weigh",
     )(own, la, lb, ra, rb, raw, edges, annealing_exponents)
 
@@ -469,7 +516,7 @@
         out_shape=S((fields, rows // ndom, cols), f32),
         in_specs=[VMEM] * ndom,
         out_specs=VMEM,
-        compiler_params=PARAMS,
+        compiler_params=params(4),
         name="join",
     )(*parts)
     blocks = [mine] + [swap(mine, k, ndom) for k in range(1, ndom)]
@@ -478,7 +525,7 @@
         out_shape=S((fields, rows, cols), f32),
         in_specs=[VMEM] * ndom,
         out_specs=VMEM,
-        compiler_params=PARAMS,
+        compiler_params=params(4),
         name="place",
     )(*blocks)
 

time: 80.8 us -> 63.4 us (0.78)
  Pallas kernels: 55.3 us -> 34 us
  local copies, waits for them, and re-layouts: 2.7 us -> 4.73 us
  waiting for transfers between devices: 9.78 us -> 11.8 us
    pallas_call x1, Pallas kernels: 14.3 us -> 7.99 us  [on_device(): pl.pallas_call(forecast_kernel, out_shape=S(ensemble.shape, f32), grid=(m...]
    pallas_call x1, Pallas kernels: 12.3 us -> 6.58 us  [on_device(): pl.pallas_call(pack_kernel, out_shape=(S((planes, fields, rows, cols), f3...]
    pallas_call x1, Pallas kernels: 10 us -> 7.31 us  [on_device(): pl.pallas_call(edge_kernel, out_shape=(S((planes, fields, rows, cols), f3...]
    pallas_call x1, Pallas kernels: 4.23 us -> 2.05 us  [on_device(): pl.pallas_call(functools.partial(own_kernel, radius=radius, cols=cols, ro...]
    unnamed x20 -> x12, local copies, waits for them, and re-layouts: 2.7 us -> 4.73 us
    ppermute x2, waiting for transfers between devices: 1.73 us -> 3.7 us  [exchange(): rb = lax.ppermute(b, 'col', outer)]
    pallas_call x1, Pallas kernels: 11.1 us -> 9.33 us  [on_device(): pl.pallas_call(functools.partial(weigh_kernel, radius=radius, parts=ndom)...]
    pallas_call x1, Pallas kernels: 1.67 us -> 0.04 us  [on_device(): pl.pallas_call(join_kernel, out_shape=S((fields, rows // ndom, cols), f32...]
  transfers between devices with their start and end apart: 10 -> 10, of which waited for: 7 -> 6; matrix products, arithmetic and copies ran while one was open for 0% -> 0% of each run, Pallas kernels for 23% -> 16%
where the time goes in v2:
time: 63.4 us; the launch traced here: 63.1 us
  Pallas kernels  34 us (54%)
  starting transfers between devices  12.5 us (20%)
  waiting for transfers between devices  11.8 us (19%)
  local copies, waits for them, and re-layouts  4.73 us (7%)
    pallas_call x1, Pallas kernels, on_device(): pl.pallas_call(functools.partial(weigh_kernel, radius=radius, parts=ndom)...  9.33 us
    ppermute x6, waiting for transfers between devices, swap(): lax.ppermute(x, 'dom', [(i, i ^ k if count & count - 1 == 0 else (i + k)...  8.07 us
    pallas_call x1, Pallas kernels, on_device(): pl.pallas_call(forecast_kernel, out_shape=S(ensemble.shape, f32), grid=(m...  7.99 us
    pallas_call x1, Pallas kernels, on_device(): pl.pallas_call(edge_kernel, out_shape=(S((planes, fields, rows, cols), f3...  7.31 us
    ppermute x6, starting transfers between devices, swap(): lax.ppermute(x, 'dom', [(i, i ^ k if count & count - 1 == 0 else (i + k)...  7.1 us
    pallas_call x1, Pallas kernels, on_device(): pl.pallas_call(pack_kernel, out_shape=(S((planes, fields, rows, cols), f3...  6.58 us
    ppermute x2, starting transfers between devices, exchange(): rb = lax.ppermute(b, 'col', outer)  4.78 us
    unnamed x12, local copies, waits for them, and re-layouts  4.73 us
  transfers between devices with their start and end apart: 10, of which 6 were waited for; matrix products, arithmetic and copies ran while one was open for 0% of the time, Pallas kernels for 16%

profile of v2, /device:TPU:0, one launch (start us, length us, event | category | flops | bytes accessed | tf_op | source)
XLA Modules:
  0.0 63.1 jit_solution(9530708596949471036)
XLA Ops:
  0.0 0.0 copy-start
  0.0 3.2 %copy-done = f32[32,5,96,128]{3,2,1,0:T(8,128)S(1)} copy-done((f32[32,5,96,128]{3,2,1,0:T(8,128)S(1)}, f32[32,5,96,128]{3,2,1,0:T(8,128)}, u32[]{:S(2)}) %copy-start) | copy-done | bytes 7864344
  3.2 0.0 copy-start.2
  3.2 0.8 %copy-done.2 = s32[96,128]{1,0:T(8,128)S(1)} copy-done((s32[96,128]{1,0:T(8,128)S(1)}, s32[96,128]{1,0:T(8,128)}, u32[]{:S(2)}) %copy-start.2) | copy-done | bytes 49176
  4.0 0.0 copy-start.4
  4.0 0.7 %copy-done.4 = s32[768]{0:T(1024)S(1)} copy-done((s32[768]{0:T(1024)S(1)}, s32[768]{0:T(1024)}, u32[]{:S(2)}) %copy-start.4) | copy-done | bytes 3096
  4.7 0.0 copy-start.1
  4.7 6.6 %pack.1 = (f32[4,5,96,128]{3,2,1,0:T(8,128)S(1)}, f32[392,128]{1,0:T(8,128)S(1)}, f32[392,128]{1,0:T(8,128)S(1)}) custom-call(f32[32,5,96,128]{3,2,1,0:T(8,128)S(1)} %copy-done, s32[96,128]{1,0:T(8,128)S(1)} %copy-done.2, s32[6,128]{1,0:T(8,128)S(1)} %bitcast.2), custom_call_target="tpu_custom_call" | custom-call | tf_op jit(solution)/shard_map/pack/pallas_call | solution.py:432
  11.3 0.6 collective-permute-start
  11.9 0.0 copy-start.5
  11.9 4.7 %collective-permute-start.1 = (f32[392,128]{1,0:T(8,128)S(1)}, f32[392,128]{1,0:T(8,128)S(1)}, u32[]{:S(2)}, u32[]{:S(2)}) collective-permute-start(f32[392,128]{1,0:T(8,128)S(1)} %get-tuple-element.15), channel_id=1, source_target_pairs={{0,7},{1,2},{2,1},{3,4},{4,3},{5,6},{6,5},{7,0},{8,15},{9,10},{10,... | collective-permute-start | bytes 602120 | tf_op jit(solution)/shard_map/ppermute | solution.py:446
  16.6 0.0 copy-done.1
  16.6 8.0 %forecast.1.x_ref = f32[32,5,96,128]{3,2,1,0:T(8,128)S(1)} custom-call(f32[32,5,96,128]{3,2,1,0:T(8,128)S(1)} %copy-done.1, s32[96,128]{1,0:T(8,128)S(1)} %copy-done.2), custom_call_target="tpu_custom_call" | custom-call | tf_op jit(solution)/shard_map/forecast/pallas_call | solution.py:452
  24.6 0.0 copy-start.3
  24.6 0.0 collective-permute-done.ra_ref
  24.6 0.0 collective-permute-done.1.rb_ref
  24.6 0.0 copy-done.5
  24.6 7.3 %edges.1 = (f32[4,5,96,128]{3,2,1,0:T(8,128)S(1)}, f32[32,768]{1,0:T(8,128)S(1)}) custom-call(f32[392,128]{1,0:T(8,128)S(1)} %collective-permute-done.ra_ref, f32[392,128]{1,0:T(8,128)S(1)} %collective-permute-done.1.rb_ref, f32[4,5,96,128]{3,2,1,0:T(8,128)S(1)} %get-tuple-element.16.g_ref, s32[96,128]{1,0:T(8,128)S(1)} %copy-done.2, ...), custom_call_target="tpu_custom_call" | custom-call | tf_op jit(solution)/shard_map/edges/pallas_call | solution.py:466
  31.9 0.1 collective-permute-start.3
  32.0 0.1 collective-permute-start.2
  32.1 2.0 %own.1.own_ref = f32[768,512]{1,0:T(8,128)S(1)} custom-call(f32[32,768]{1,0:T(8,128)S(1)} %get-tuple-element.17.loss_ref, s32[6,128]{1,0:T(8,128)S(1)} %bitcast.4), custom_call_target="tpu_custom_call" | custom-call | tf_op jit(solution)/shard_map/own/pallas_call | solution.py:485
  34.1 3.7 %collective-permute-done.3.lb_ref = f32[32,768]{1,0:T(8,128)S(1)} collective-permute-done((f32[32,768]{1,0:T(8,128)S(1)}, f32[32,768]{1,0:T(8,128)S(1)}, u32[]{:S(2)}, u32[]{:S(2)}) %collective-permute-start.3) | collective-permute-done | bytes 98336 | tf_op jit(solution)/shard_map/ppermute | solution.py:446
  37.8 0.0 collective-permute-done.2.la_ref
  37.8 0.0 copy-done.3
  37.8 9.3 %weigh.1 = (f32[7,24,128]{2,1,0:T(8,128)S(1)}, f32[7,24,128]{2,1,0:T(8,128)S(1)}, f32[7,24,128]{2,1,0:T(8,128)S(1)}, f32[7,24,128]{2,1,0:T(8,128)S(1)}) custom-call(f32[768,512]{1,0:T(8,128)S(1)} %own.1.own_ref, f32[32,768]{1,0:T(8,128)S(1)} %collective-permute-done.2.la_ref, f32[32,768]{1,0:T(8,128)S(1)} %collective-permute-done.3.lb_ref, ...), custom_call_target="tpu_custom_call" | custom-call | tf_op jit(solution)/shard_map/weigh/pallas_call | solution.py:496
  47.2 1.6 %collective-permute-start.4 = (f32[7,24,128]{2,1,0:T(8,128)S(1)}, f32[7,24,128]{2,1,0:T(8,128)S(1)}, u32[]{:S(2)}, u32[]{:S(2)}) collective-permute-start(f32[7,24,128]{2,1,0:T(8,128)S(1)} %get-tuple-element.20), channel_id=1, source_target_pairs={{0,8},{8,0},{16,24},{24,16},{1,9},{9,1},{17,25},{25,17},{2,10},{10... | collective-permute-start | bytes 258056 | tf_op jit(solution)/shard_map/ppermute | solution.py:391
  48.7 1.5 %collective-permute-start.5 = (f32[7,24,128]{2,1,0:T(8,128)S(1)}, f32[7,24,128]{2,1,0:T(8,128)S(1)}, u32[]{:S(2)}, u32[]{:S(2)}) collective-permute-start(f32[7,24,128]{2,1,0:T(8,128)S(1)} %get-tuple-element.21), channel_id=1, source_target_pairs={{0,16},{8,24},{16,0},{24,8},{1,17},{9,25},{17,1},{25,9},{2,18},{10... | collective-permute-start | bytes 258056 | tf_op jit(solution)/shard_map/ppermute | solution.py:391
  50.3 0.5 collective-permute-start.6
  50.7 1.0 %collective-permute-done.4.refs_1_ = f32[7,24,128]{2,1,0:T(8,128)S(1)} collective-permute-done((f32[7,24,128]{2,1,0:T(8,128)S(1)}, f32[7,24,128]{2,1,0:T(8,128)S(1)}, u32[]{:S(2)}, u32[]{:S(2)}) %collective-permute-start.4) | collective-permute-done | bytes 86048 | tf_op jit(solution)/shard_map/ppermute | solution.py:391
  51.7 1.5 %collective-permute-done.5.refs_2_ = f32[7,24,128]{2,1,0:T(8,128)S(1)} collective-permute-done((f32[7,24,128]{2,1,0:T(8,128)S(1)}, f32[7,24,128]{2,1,0:T(8,128)S(1)}, u32[]{:S(2)}, u32[]{:S(2)}) %collective-permute-start.5) | collective-permute-done | bytes 86048 | tf_op jit(solution)/shard_map/ppermute | solution.py:391
  53.2 3.3 %collective-permute-done.6.refs_3_ = f32[7,24,128]{2,1,0:T(8,128)S(1)} collective-permute-done((f32[7,24,128]{2,1,0:T(8,128)S(1)}, f32[7,24,128]{2,1,0:T(8,128)S(1)}, u32[]{:S(2)}, u32[]{:S(2)}) %collective-permute-start.6) | collective-permute-done | bytes 86048 | tf_op jit(solution)/shard_map/ppermute | solution.py:391
  56.6 0.1 collective-permute-start.9
  56.7 1.5 %collective-permute-start.8 = (f32[5,24,128]{2,1,0:T(8,128)S(1)}, f32[5,24,128]{2,1,0:T(8,128)S(1)}, u32[]{:S(2)}, u32[]{:S(2)}) collective-permute-start(f32[5,24,128]{2,1,0:T(8,128)S(1)} %join.1.refs_0_), channel_id=1, source_target_pairs={{0,16},{8,24},{16,0},{24,8},{1,17},{9,25},{17,1},{25,9},{2,18},{10... | collective-permute-start | bytes 184328 | tf_op jit(solution)/shard_map/ppermute | solution.py:391
  58.2 2.0 %collective-permute-start.7 = (f32[5,24,128]{2,1,0:T(8,128)S(1)}, f32[5,24,128]{2,1,0:T(8,128)S(1)}, u32[]{:S(2)}, u32[]{:S(2)}) collective-permute-start(f32[5,24,128]{2,1,0:T(8,128)S(1)} %join.1.refs_0_), channel_id=1, source_target_pairs={{0,8},{8,0},{16,24},{24,16},{1,9},{9,1},{17,25},{25,17},{2,10},{10... | collective-permute-start | bytes 184328 | tf_op jit(solution)/shard_map/ppermute | solution.py:391
  60.2 1.6 %collective-permute-done.9.refs_3_ = f32[5,24,128]{2,1,0:T(8,128)S(1)} collective-permute-done((f32[5,24,128]{2,1,0:T(8,128)S(1)}, f32[5,24,128]{2,1,0:T(8,128)S(1)}, u32[]{:S(2)}, u32[]{:S(2)}) %collective-permute-start.9) | collective-permute-done | bytes 61472 | tf_op jit(solution)/shard_map/ppermute | solution.py:391
  61.8 0.0 collective-permute-done.8.refs_2_
  61.8 0.6 collective-permute-done.7.refs_1_
  62.4 0.7 %place.1 = f32[5,96,128]{2,1,0:T(8,128)} custom-call(f32[5,24,128]{2,1,0:T(8,128)S(1)} %join.1.refs_0_, f32[5,24,128]{2,1,0:T(8,128)S(1)} %collective-permute-done.7.refs_1_, f32[5,24,128]{2,1,0:T(8,128)S(1)} %collective-permute-done.8.refs_2_, f32[5,24,128]{2,1,0:T(8,128)S(1)} %collective-permute-done.9.refs_3_), custom_call_target="tpu_custom_call" | custom-call | tf_op jit(solution)/shard_map/place/pallas_call | solution.py:523
  (1 shorter events, 0.0 us)
Async XLA Ops:
  0.0 3.2 %copy-start = (f32[32,5,96,128]{3,2,1,0:T(8,128)S(1)}, f32[32,5,96,128]{3,2,1,0:T(8,128)}, u32[]{:S(2)}) copy-start(f32[32,5,96,128]{3,2,1,0:T(8,128)} %x_ref.1) | copy-start | bytes 23592964
  3.2 0.8 %copy-start.2 = (s32[96,128]{1,0:T(8,128)S(1)}, s32[96,128]{1,0:T(8,128)}, u32[]{:S(2)}) copy-start(s32[96,128]{1,0:T(8,128)} %cls_ref.5) | copy-start | bytes 147460
  4.0 0.7 %copy-start.4 = (s32[768]{0:T(1024)S(1)}, s32[768]{0:T(1024)}, u32[]{:S(2)}) copy-start(s32[768]{0:T(1024)} %param.7) | copy-start | bytes 9220
  4.7 11.9 %copy-start.1 = (f32[32,5,96,128]{3,2,1,0:T(8,128)S(1)}, f32[32,5,96,128]{3,2,1,0:T(8,128)}, u32[]{:S(2)}) copy-start(f32[32,5,96,128]{3,2,1,0:T(8,128)} %x_ref.1) | copy-start | bytes 23592964
  11.3 13.3 %collective-permute-start = (f32[392,128]{1,0:T(8,128)S(1)}, f32[392,128]{1,0:T(8,128)S(1)}, u32[]{:S(2)}, u32[]{:S(2)}) collective-permute-start(f32[392,128]{1,0:T(8,128)S(1)} %get-tuple-element.14), channel_id=1, source_target_pairs={{0,1},{1,0},{2,3},{3,2},{4,5},{5,4},{6,7},{7,6},{8,9},{9,8},{10,11... | collective-permute-start | bytes 602120 | tf_op jit(solution)/shard_map/ppermute | solution.py:447
  11.9 12.7 %copy-start.5 = (f32[768]{0:T(1024)S(1)}, f32[768]{0:T(1024)}, u32[]{:S(2)}) copy-start(f32[768]{0:T(1024)} %param.8) | copy-start | bytes 9220
  11.9 12.7 %collective-permute-start.1 = (f32[392,128]{1,0:T(8,128)S(1)}, f32[392,128]{1,0:T(8,128)S(1)}, u32[]{:S(2)}, u32[]{:S(2)}) collective-permute-start(f32[392,128]{1,0:T(8,128)S(1)} %get-tuple-element.15), channel_id=1, source_target_pairs={{0,7},{1,2},{2,1},{3,4},{4,3},{5,6},{6,5},{7,0},{8,15},{9,10},{10,... | collective-permute-start | bytes 602120 | tf_op jit(solution)/shard_map/ppermute | solution.py:446
  24.6 13.3 %copy-start.3 = (f32[96,128]{1,0:T(8,128)S(1)}, f32[96,128]{1,0:T(8,128)}, u32[]{:S(2)}) copy-start(f32[96,128]{1,0:T(8,128)} %ann_ref.1) | copy-start | bytes 147460
  31.9 5.9 %collective-permute-start.3 = (f32[32,768]{1,0:T(8,128)S(1)}, f32[32,768]{1,0:T(8,128)S(1)}, u32[]{:S(2)}, u32[]{:S(2)}) collective-permute-start(f32[32,768]{1,0:T(8,128)S(1)} %get-tuple-element.17.loss_ref), channel_id=1, source_target_pairs={{0,7},{1,2},{2,1},{3,4},{4,3},{5,6},{6,5},{7,0},{8,15},{9,10},{10,... | collective-permute-start | bytes 294920 | tf_op jit(solution)/shard_map/ppermute | solution.py:446
  32.0 5.8 %collective-permute-start.2 = (f32[32,768]{1,0:T(8,128)S(1)}, f32[32,768]{1,0:T(8,128)S(1)}, u32[]{:S(2)}, u32[]{:S(2)}) collective-permute-start(f32[32,768]{1,0:T(8,128)S(1)} %get-tuple-element.17.loss_ref), channel_id=1, source_target_pairs={{0,1},{1,0},{2,3},{3,2},{4,5},{5,4},{6,7},{7,6},{8,9},{9,8},{10,11... | collective-permute-start | bytes 294920 | tf_op jit(solution)/shard_map/ppermute | solution.py:447
  47.2 4.6 %collective-permute-start.4 = (f32[7,24,128]{2,1,0:T(8,128)S(1)}, f32[7,24,128]{2,1,0:T(8,128)S(1)}, u32[]{:S(2)}, u32[]{:S(2)}) collective-permute-start(f32[7,24,128]{2,1,0:T(8,128)S(1)} %get-tuple-element.20), channel_id=1, source_target_pairs={{0,8},{8,0},{16,24},{24,16},{1,9},{9,1},{17,25},{25,17},{2,10},{10... | collective-permute-start | bytes 258056 | tf_op jit(solution)/shard_map/ppermute | solution.py:391
  48.7 4.5 %collective-permute-start.5 = (f32[7,24,128]{2,1,0:T(8,128)S(1)}, f32[7,24,128]{2,1,0:T(8,128)S(1)}, u32[]{:S(2)}, u32[]{:S(2)}) collective-permute-start(f32[7,24,128]{2,1,0:T(8,128)S(1)} %get-tuple-element.21), channel_id=1, source_target_pairs={{0,16},{8,24},{16,0},{24,8},{1,17},{9,25},{17,1},{25,9},{2,18},{10... | collective-permute-start | bytes 258056 | tf_op jit(solution)/shard_map/ppermute | solution.py:391
  50.3 6.3 %collective-permute-start.6 = (f32[7,24,128]{2,1,0:T(8,128)S(1)}, f32[7,24,128]{2,1,0:T(8,128)S(1)}, u32[]{:S(2)}, u32[]{:S(2)}) collective-permute-start(f32[7,24,128]{2,1,0:T(8,128)S(1)} %get-tuple-element.22), channel_id=1, source_target_pairs={{0,24},{8,16},{16,8},{24,0},{1,25},{9,17},{17,9},{25,1},{2,26},{10... | collective-permute-start | bytes 258056 | tf_op jit(solution)/shard_map/ppermute | solution.py:391
  56.6 5.2 %collective-permute-start.9 = (f32[5,24,128]{2,1,0:T(8,128)S(1)}, f32[5,24,128]{2,1,0:T(8,128)S(1)}, u32[]{:S(2)}, u32[]{:S(2)}) collective-permute-start(f32[5,24,128]{2,1,0:T(8,128)S(1)} %join.1.refs_0_), channel_id=1, source_target_pairs={{0,24},{8,16},{16,8},{24,0},{1,25},{9,17},{17,9},{25,1},{2,26},{10... | collective-permute-start | bytes 184328 | tf_op jit(solution)/shard_map/ppermute | solution.py:391
  56.7 5.1 %collective-permute-start.8 = (f32[5,24,128]{2,1,0:T(8,128)S(1)}, f32[5,24,128]{2,1,0:T(8,128)S(1)}, u32[]{:S(2)}, u32[]{:S(2)}) collective-permute-start(f32[5,24,128]{2,1,0:T(8,128)S(1)} %join.1.refs_0_), channel_id=1, source_target_pairs={{0,16},{8,24},{16,0},{24,8},{1,17},{9,25},{17,1},{25,9},{2,18},{10... | collective-permute-start | bytes 184328 | tf_op jit(solution)/shard_map/ppermute | solution.py:391
  58.2 4.2 %collective-permute-start.7 = (f32[5,24,128]{2,1,0:T(8,128)S(1)}, f32[5,24,128]{2,1,0:T(8,128)S(1)}, u32[]{:S(2)}, u32[]{:S(2)}) collective-permute-start(f32[5,24,128]{2,1,0:T(8,128)S(1)} %join.1.refs_0_), channel_id=1, source_target_pairs={{0,8},{8,0},{16,24},{24,16},{1,9},{9,1},{17,25},{25,17},{2,10},{10... | collective-permute-start | bytes 184328 | tf_op jit(solution)/shard_map/ppermute | solution.py:391

commit v3 on v2

--- a/solution.py
+++ b/solution.py
@@ -78,12 +78,14 @@
     return step(step(fields, depth, pad, slot, table), depth, pad, slot + 4, table)
 
 
-def pack_kernel(x_hbm, cls_ref, idx_ref, g_ref, pa_ref, pb_ref, buf, sem):
+def pack_kernel(x_hbm, cls_hbm, idx_hbm, g_ref, pa_ref, pb_ref, buf, cls_ref, idx_ref, sem):
     members, fields, rows, cols = x_hbm.shape
     per = cols // GROUP
     planes = members // per
     even = lax.rem(lax.axis_index("col"), 2) == 0
     copies = [pltpu.make_async_copy(x_hbm.at[:, f], buf.at[f], sem.at[f]) for f in range(fields)]
+    copies.append(pltpu.make_async_copy(cls_hbm, cls_ref, sem.at[fields]))
+    copies.append(pltpu.make_async_copy(idx_hbm, idx_ref, sem.at[fields + 1]))
     for c in copies:
         c.start()
 
@@ -114,6 +116,8 @@
 
     for f in range(3):
         copies[f].wait()
+        if f == 1:
+            copies[fields].wait()
 
         def body(t, carry, f=f):
             right, left = edges(f, t)
@@ -137,6 +141,7 @@
         return carry
 
     lax.fori_loop(0, rows // 8, tracers, 0, unroll=2)
+    copies[fields + 1].wait()
     n = idx_ref.shape[0]
     for ref in (pa_ref, pb_ref):
         ref[4 * rows : 4 * rows + 8, :] = jnp.zeros((8, cols), f32)
@@ -148,12 +153,12 @@
     pl.when(pl.program_id(0) == 0)(lambda: prepare(pad, table))
 
     def body(m, carry):
-        out = two_steps([x_ref[m, f] for f in range(5)], depth, pad, table)
+        out = two_steps([x_ref[f, m] for f in range(5)], depth, pad, table)
         for f in range(5):
             o_ref[m, f] = out[f]
         return carry
 
-    lax.fori_loop(0, x_ref.shape[0], body, 0, unroll=4)
+    lax.fori_loop(0, o_ref.shape[0], body, 0, unroll=4)
 
 
 def pieces_of(x):
@@ -168,7 +173,7 @@
     return jnp.concatenate([x[i : i + 1, :] for i in range(x.shape[0])], axis=1)
 
 
-def edge_kernel(ra_ref, rb_ref, g_ref, cls_ref, x_ref, idx_ref, obs_ref, z_ref, loss_ref, xs, pad, table, lhs, low, prod):
+def edge_kernel(ra_ref, rb_ref, g_ref, cls_ref, x_ref, idx_ref, obs_ref, z_ref, loss_ref, xs, pad, table, lhs, pick, prod):
     members, _, rows, cols = x_ref.shape
     per = cols // GROUP
     planes = members // per
@@ -188,10 +193,9 @@
         r = roll_lanes(depth, GROUP * i + HALF)
         tiled = r if tiled is None else jnp.where(grp == i, r, tiled)
     ul, ur = received(1)
-    dl = roll_lanes(tiled, -EDGE)
-    dr = tiled
+    dl = dr = tiled
     for n in range(3):
-        dl = jnp.where(j == n + 1, jnp.broadcast_to(ul[:, EDGE * n : EDGE * n + 1], dl.shape), dl)
+        dl = jnp.where(j == EDGE + n + 1, jnp.broadcast_to(ul[:, EDGE * n : EDGE * n + 1], dl.shape), dl)
         dr = jnp.where(j == HALF + n, jnp.broadcast_to(ur[:, EDGE * n + 3 : EDGE * n + 4], dr.shape), dr)
     xs[0, 5] = dl
     xs[1, 5] = dr
@@ -207,15 +211,14 @@
         right = []
         for f in range(5):
             g = g_ref[q, f]
-            hl = pltpu.roll(xs[0, f], lax.rem(cols - EDGE * q, cols), 1)
+            hl = pltpu.roll(xs[0, f], lax.rem(cols + EDGE - EDGE * q, cols), 1)
             hr = pltpu.roll(xs[1, f], lax.rem(cols + HALF - EDGE * q, cols), 1)
-            left.append(jnp.where(j < EDGE, hl, roll_lanes(g, -EDGE)))
+            left.append(jnp.where((j >= EDGE) & (j < HALF), hl, g))
             right.append(jnp.where(j >= HALF, hr, g))
         left = two_steps(left, xs[0, 5], pad, table)
         right = two_steps(right, xs[1, 5], pad, table, 8)
-        inner = (j >= EDGE) & (j < 2 * EDGE)
         for f in range(5):
-            z_ref[q, f] = jnp.where(inner, right[f], roll_lanes(left[f], EDGE))
+            z_ref[q, f] = jnp.where(j < HALF, right[f], left[f])
         return carry
 
     prepare(pad, table)
@@ -225,26 +228,35 @@
     obs = row_vector(obs_ref[...])
     nobs = idx.shape[1]
     row, col = lax.shift_right_logical(idx, cols.bit_length() - 1), idx & (cols - 1)
-    pick = (lax.broadcasted_iota(jnp.int32, (cols, nobs), 0) == col).astype(f32).astype(bf16)
-    pick2 = jnp.concatenate([pick, pick], axis=0)
-    isrow = lax.broadcasted_iota(jnp.int32, (rows, nobs), 0) == row
+    band = rows // BANDS
+    block = sum(jnp.where(row >= band * b, 1, 0) for b in range(1, BANDS))
+    here = lax.broadcasted_iota(jnp.int32, (cols, nobs), 0) == col
+    for b in range(BANDS):
+        pick[b * cols : (b + 1) * cols, :] = jnp.where(here & (block == b), 1.0, 0.0).astype(bf16)
+    isrow = lax.broadcasted_iota(jnp.int32, (band, nobs), 0) == row - band * block
     border = (lane < EDGE) | (lane >= cols - EDGE)
 
+    def split(q, carry):
+        for i in range(0, per, 2):
+            pair = [
+                jnp.where(border, roll_lanes(z_ref[q, 0], cols - HALF - GROUP * n), x_ref[q * per + n, 0])
+                for n in (i, i + 1)
+            ]
+            at = pl.ds(pl.multiple_of((q * per + i) * band, 16), 2 * band)
+            for b in range(BANDS):
+                both = jnp.concatenate([h[b * band : (b + 1) * band] for h in pair], axis=0)
+                for p, piece in enumerate(pieces_of(both)):
+                    lhs[p, at, b * cols : (b + 1) * cols] = piece
+        return carry
+
+    lax.fori_loop(0, planes, split, 0)
+    prod[...] = sum(jnp.dot(lhs[p], pick[...], preferred_element_type=f32) for p in range(3))
+
     def gather(q, carry):
+        ys = []
         for i in range(per):
-            at = slice(i * rows, (i + 1) * rows)
-            h = jnp.where(border, roll_lanes(z_ref[q, 0], cols - HALF - GROUP * i), x_ref[q * per + i, 0])
-            hi, mid, lo = pieces_of(h)
-            lhs[at, :cols] = hi
-            lhs[at, cols:] = mid
-            low[at, :] = lo
-        prod[...] = jnp.dot(lhs[...], pick2, preferred_element_type=f32) + jnp.dot(
-            low[...], pick, preferred_element_type=f32
-        )
-        ys = [
-            jnp.sum(jnp.where(isrow, prod[i * rows : (i + 1) * rows, :], 0.0), axis=0, keepdims=True)
-            for i in range(per)
-        ]
+            at = pl.ds(pl.multiple_of((q * per + i) * band, 8), band)
+            ys.append(jnp.sum(jnp.where(isrow, prod[at, :], 0.0), axis=0, keepdims=True))
         misfit = obs - jnp.concatenate(ys, axis=0)
         loss_ref[pl.ds(pl.multiple_of(q * per, 8), per), :] = -0.5 * misfit * misfit
         return carry
@@ -375,7 +387,7 @@
         tot[fields, at, :] = total
         return carry
 
-    lax.fori_loop(0, rows // 8, sums, 0)
+    lax.fori_loop(0, rows // 8, sums, 0, unroll=2)
     part = rows // parts
     me = lax.axis_index("dom")
     for k, ref in enumerate(outs):
@@ -422,6 +434,7 @@
     per = cols // GROUP
     planes = members // per
     nobs = obs_index.shape[0]
+    tall = members * rows // BANDS
     ncol = lax.axis_size("col")
     ndom = lax.axis_size("dom")
     S = jax.ShapeDtypeStruct
@@ -429,15 +442,19 @@
     obs = obs_value.reshape(nobs // cols, cols)
 
     payload = S((4 * rows + 8, cols), f32)
-    packed, pa, pb = pl.pallas_call(
+    packed, pa, pb, held = pl.pallas_call(
         pack_kernel,
-        out_shape=(S((planes, fields, rows, cols), f32), payload, payload),
-        in_specs=[HBM, VMEM, VMEM],
-        out_specs=(VMEM, VMEM, VMEM),
-        scratch_shapes=[pltpu.VMEM((fields, members, rows, cols), f32), pltpu.SemaphoreType.DMA((fields,))],
-        compiler_params=params(14),
+        out_shape=(S((planes, fields, rows, cols), f32), payload, payload, S((fields, members, rows, cols), f32)),
+        in_specs=[HBM] * 3,
+        out_specs=(VMEM,) * 4,
+        scratch_shapes=[
+            pltpu.VMEM(depth_class.shape, jnp.int32),
+            pltpu.VMEM(idx.shape, jnp.int32),
+            pltpu.SemaphoreType.DMA((fields + 2,)),
+        ],
+        compiler_params=params(44),
         name="pack",
-    )(ensemble, depth_class, idx)
+    )(*[pltpu.with_memory_space_constraint(x, pltpu.HBM) for x in (ensemble, depth_class, idx)])
 
     inner = [(i, i ^ 1) for i in range(ncol)]
     outer = [(i, (i + 1) % ncol if i % 2 else (i - 1) % ncol) for i in range(ncol)]
@@ -454,14 +471,14 @@
         out_shape=S(ensemble.shape, f32),
         grid=(members // block,),
         in_specs=[
-            pl.BlockSpec((block, fields, rows, cols), lambda m: (m, 0, 0, 0)),
+            pl.BlockSpec((fields, block, rows, cols), lambda m: (0, m, 0, 0)),
             pl.BlockSpec((rows, cols), lambda m: (0, 0)),
         ],
         out_specs=pl.BlockSpec((block, fields, rows, cols), lambda m: (m, 0, 0, 0)),
         scratch_shapes=[pltpu.VMEM((8, rows + 2 * ZEROS, cols), f32), pltpu.VMEM((2 * cols, cols), bf16)],
         compiler_params=params(12),
         name="forecast",
-    )(ensemble, depth_class)
+    )(held, depth_class)
 
     edges, loss = pl.pallas_call(
         edge_kernel,
@@ -472,16 +489,15 @@
             pltpu.VMEM((2, fields + 1, rows, cols), f32),
             pltpu.VMEM((16, rows + 2 * ZEROS, cols), f32),
             pltpu.VMEM((2 * cols, cols), bf16),
-            pltpu.VMEM((per * rows, 2 * cols), bf16),
-            pltpu.VMEM((per * rows, cols), bf16),
-            pltpu.VMEM((per * rows, nobs), f32),
+            pltpu.VMEM((3, tall, BANDS * cols), bf16),
+            pltpu.VMEM((BANDS * cols, nobs), bf16),
+            pltpu.VMEM((tall, nobs), f32),
         ],
         compiler_params=params(18),
         name="edges",
     )(ra, rb, packed, depth_class, raw, idx, obs)
 
     la, lb = exchange(loss, loss)
-    tall = members * rows // BANDS
     own = pl.pallas_call(
         functools.partial(own_kernel, radius=radius, cols=cols, rows=rows),
         out_shape=S((tall, BANDS * cols), f32),
@@ -504,7 +520,7 @@
             pltpu.VMEM((2, tall, BANDS * cols // 2), f32),
             pltpu.VMEM((members, rows, cols), f32),
             pltpu.VMEM((fields + 2, rows, cols), f32),
-            pltpu.VMEM((2, 4, rows + 4 * ZEROS, cols), f32),
+            pltpu.VMEM((4, 4, rows + 4 * ZEROS, cols), f32),
         ],
         compiler_params=params(30),
         name="weigh",

time: 63.4 us -> 56.5 us (0.89)
  local copies, waits for them, and re-layouts: 4.73 us -> 0.02 us
  Pallas kernels: 34 us -> 32 us
    unnamed x12 -> x8, local copies, waits for them, and re-layouts: 4.73 us -> 0.02 us
    pallas_call x1, Pallas kernels: 9.33 us -> 6.56 us  [on_device(): pl.pallas_call(functools.partial(weigh_kernel, radius=radius, parts=ndom)...]
    pallas_call x1, Pallas kernels: 6.58 us -> 7.98 us  [on_device(): pl.pallas_call(pack_kernel, out_shape=(S((planes, fields, rows, cols), f3...]
    pallas_call x1, Pallas kernels: 7.31 us -> 6.33 us  [on_device(): pl.pallas_call(edge_kernel, out_shape=(S((planes, fields, rows, cols), f3...]
  transfers between devices with their start and end apart: 10 -> 10, of which waited for: 6 -> 6; matrix products, arithmetic and copies ran while one was open for 0% -> 0% of each run, Pallas kernels for 16% -> 18%
where the time goes in v3:
time: 56.5 us; the launch traced here: 56.4 us
  Pallas kernels  32 us (57%)
  starting transfers between devices  12.5 us (22%)
  waiting for transfers between devices  11.8 us (21%)
    pallas_call x1, Pallas kernels, on_device(): pl.pallas_call(forecast_kernel, out_shape=S(ensemble.shape, f32), grid=(m...  8.29 us
    ppermute x6, waiting for transfers between devices, swap(): lax.ppermute(x, 'dom', [(i, i ^ k if count & count - 1 == 0 else (i + k)...  8.07 us
    pallas_call x1, Pallas kernels, on_device(): pl.pallas_call(pack_kernel, out_shape=(S((planes, fields, rows, cols), f3...  7.98 us
    ppermute x6, starting transfers between devices, swap(): lax.ppermute(x, 'dom', [(i, i ^ k if count & count - 1 == 0 else (i + k)...  7.1 us
    pallas_call x1, Pallas kernels, on_device(): pl.pallas_call(functools.partial(weigh_kernel, radius=radius, parts=ndom)...  6.56 us
    pallas_call x1, Pallas kernels, on_device(): pl.pallas_call(edge_kernel, out_shape=(S((planes, fields, rows, cols), f3...  6.33 us
    ppermute x2, starting transfers between devices, exchange(): rb = lax.ppermute(b, 'col', outer)  4.78 us
    ppermute x2, waiting for transfers between devices, exchange(): rb = lax.ppermute(b, 'col', outer)  3.7 us
  transfers between devices with their start and end apart: 10, of which 6 were waited for; matrix products, arithmetic and copies ran while one was open for 0% of the time, Pallas kernels for 18%

profile of v3, /device:TPU:0, one launch (start us, length us, event | category | flops | bytes accessed | tf_op | source)
XLA Modules:
  0.0 56.4 jit_solution(15093050175526688286)
XLA Ops:
  0.0 0.0 copy-start
  0.0 8.0 %pack.1 = (f32[4,5,96,128]{3,2,1,0:T(8,128)S(1)}, f32[392,128]{1,0:T(8,128)S(1)}, f32[392,128]{1,0:T(8,128)S(1)}, f32[5,32,96,128]{3,2,1,0:T(8,128)S(1)}) custom-call(f32[32,5,96,128]{3,2,1,0:T(8,128)} %x_hbm.1, s32[96,128]{1,0:T(8,128)} %cls_ref.3, s32[6,128]{1,0:T(8,128)} %bitcast.2), custom_call_target="tpu_custom_call" | custom-call | tf_op jit(solution)/shard_map/pack/pallas_call | solution.py:445
  8.0 0.6 collective-permute-start
  8.6 4.7 %collective-permute-start.1 = (f32[392,128]{1,0:T(8,128)S(1)}, f32[392,128]{1,0:T(8,128)S(1)}, u32[]{:S(2)}, u32[]{:S(2)}) collective-permute-start(f32[392,128]{1,0:T(8,128)S(1)} %get-tuple-element.16), channel_id=1, source_target_pairs={{0,7},{1,2},{2,1},{3,4},{4,3},{5,6},{6,5},{7,0},{8,15},{9,10},{10,... | collective-permute-start | bytes 602120 | tf_op jit(solution)/shard_map/ppermute | solution.py:463
  13.3 0.0 copy-done
  13.3 0.0 copy-start.2
  13.3 0.0 copy-start.3
  13.3 8.3 %forecast.1.x_ref = f32[32,5,96,128]{3,2,1,0:T(8,128)S(1)} custom-call(f32[5,32,96,128]{3,2,1,0:T(8,128)S(1)} %get-tuple-element.18.x_ref, s32[96,128]{1,0:T(8,128)S(1)} %copy-done), custom_call_target="tpu_custom_call" | custom-call | tf_op jit(solution)/shard_map/forecast/pallas_call | solution.py:469
  21.6 0.0 copy-start.1
  21.6 0.0 collective-permute-done.ra_ref
  21.6 0.0 collective-permute-done.1.rb_ref
  21.6 0.0 copy-done.2
  21.6 0.0 copy-done.3
  21.6 6.3 %edges.1 = (f32[4,5,96,128]{3,2,1,0:T(8,128)S(1)}, f32[32,768]{1,0:T(8,128)S(1)}) custom-call(f32[392,128]{1,0:T(8,128)S(1)} %collective-permute-done.ra_ref, f32[392,128]{1,0:T(8,128)S(1)} %collective-permute-done.1.rb_ref, f32[4,5,96,128]{3,2,1,0:T(8,128)S(1)} %get-tuple-element.17.g_ref, s32[96,128]{1,0:T(8,128)S(1)} %copy-done, ...), custom_call_target="tpu_custom_call" | custom-call | tf_op jit(solution)/shard_map/edges/pallas_call | solution.py:483
  27.9 0.1 collective-permute-start.3
  28.0 0.1 collective-permute-start.2
  28.1 2.0 %own.1.own_ref = f32[768,512]{1,0:T(8,128)S(1)} custom-call(f32[32,768]{1,0:T(8,128)S(1)} %get-tuple-element.19.loss_ref, s32[6,128]{1,0:T(8,128)S(1)} %bitcast.4), custom_call_target="tpu_custom_call" | custom-call | tf_op jit(solution)/shard_map/own/pallas_call | solution.py:501
  30.1 3.7 %collective-permute-done.3.lb_ref = f32[32,768]{1,0:T(8,128)S(1)} collective-permute-done((f32[32,768]{1,0:T(8,128)S(1)}, f32[32,768]{1,0:T(8,128)S(1)}, u32[]{:S(2)}, u32[]{:S(2)}) %collective-permute-start.3) | collective-permute-done | bytes 98336 | tf_op jit(solution)/shard_map/ppermute | solution.py:463
  33.8 0.0 collective-permute-done.2.la_ref
  33.8 0.0 copy-done.1
  33.9 6.6 %weigh.1 = (f32[7,24,128]{2,1,0:T(8,128)S(1)}, f32[7,24,128]{2,1,0:T(8,128)S(1)}, f32[7,24,128]{2,1,0:T(8,128)S(1)}, f32[7,24,128]{2,1,0:T(8,128)S(1)}) custom-call(f32[768,512]{1,0:T(8,128)S(1)} %own.1.own_ref, f32[32,768]{1,0:T(8,128)S(1)} %collective-permute-done.2.la_ref, f32[32,768]{1,0:T(8,128)S(1)} %collective-permute-done.3.lb_ref, ...), custom_call_target="tpu_custom_call" | custom-call | tf_op jit(solution)/shard_map/weigh/pallas_call | solution.py:512
  40.4 1.6 %collective-permute-start.4 = (f32[7,24,128]{2,1,0:T(8,128)S(1)}, f32[7,24,128]{2,1,0:T(8,128)S(1)}, u32[]{:S(2)}, u32[]{:S(2)}) collective-permute-start(f32[7,24,128]{2,1,0:T(8,128)S(1)} %get-tuple-element.22), channel_id=1, source_target_pairs={{0,8},{8,0},{16,24},{24,16},{1,9},{9,1},{17,25},{25,17},{2,10},{10... | collective-permute-start | bytes 258056 | tf_op jit(solution)/shard_map/ppermute | solution.py:403
  42.0 1.5 %collective-permute-start.5 = (f32[7,24,128]{2,1,0:T(8,128)S(1)}, f32[7,24,128]{2,1,0:T(8,128)S(1)}, u32[]{:S(2)}, u32[]{:S(2)}) collective-permute-start(f32[7,24,128]{2,1,0:T(8,128)S(1)} %get-tuple-element.23), channel_id=1, source_target_pairs={{0,16},{8,24},{16,0},{24,8},{1,17},{9,25},{17,1},{25,9},{2,18},{10... | collective-permute-start | bytes 258056 | tf_op jit(solution)/shard_map/ppermute | solution.py:403
  43.5 0.5 collective-permute-start.6
  44.0 1.0 %collective-permute-done.4.refs_1_ = f32[7,24,128]{2,1,0:T(8,128)S(1)} collective-permute-done((f32[7,24,128]{2,1,0:T(8,128)S(1)}, f32[7,24,128]{2,1,0:T(8,128)S(1)}, u32[]{:S(2)}, u32[]{:S(2)}) %collective-permute-start.4) | collective-permute-done | bytes 86048 | tf_op jit(solution)/shard_map/ppermute | solution.py:403
  45.0 1.5 %collective-permute-done.5.refs_2_ = f32[7,24,128]{2,1,0:T(8,128)S(1)} collective-permute-done((f32[7,24,128]{2,1,0:T(8,128)S(1)}, f32[7,24,128]{2,1,0:T(8,128)S(1)}, u32[]{:S(2)}, u32[]{:S(2)}) %collective-permute-start.5) | collective-permute-done | bytes 86048 | tf_op jit(solution)/shard_map/ppermute | solution.py:403
  46.5 3.3 %collective-permute-done.6.refs_3_ = f32[7,24,128]{2,1,0:T(8,128)S(1)} collective-permute-done((f32[7,24,128]{2,1,0:T(8,128)S(1)}, f32[7,24,128]{2,1,0:T(8,128)S(1)}, u32[]{:S(2)}, u32[]{:S(2)}) %collective-permute-start.6) | collective-permute-done | bytes 86048 | tf_op jit(solution)/shard_map/ppermute | solution.py:403
  49.8 0.1 collective-permute-start.9
  49.9 1.5 %collective-permute-start.8 = (f32[5,24,128]{2,1,0:T(8,128)S(1)}, f32[5,24,128]{2,1,0:T(8,128)S(1)}, u32[]{:S(2)}, u32[]{:S(2)}) collective-permute-start(f32[5,24,128]{2,1,0:T(8,128)S(1)} %join.1.refs_0_), channel_id=1, source_target_pairs={{0,16},{8,24},{16,0},{24,8},{1,17},{9,25},{17,1},{25,9},{2,18},{10... | collective-permute-start | bytes 184328 | tf_op jit(solution)/shard_map/ppermute | solution.py:403
  51.4 2.0 %collective-permute-start.7 = (f32[5,24,128]{2,1,0:T(8,128)S(1)}, f32[5,24,128]{2,1,0:T(8,128)S(1)}, u32[]{:S(2)}, u32[]{:S(2)}) collective-permute-start(f32[5,24,128]{2,1,0:T(8,128)S(1)} %join.1.refs_0_), channel_id=1, source_target_pairs={{0,8},{8,0},{16,24},{24,16},{1,9},{9,1},{17,25},{25,17},{2,10},{10... | collective-permute-start | bytes 184328 | tf_op jit(solution)/shard_map/ppermute | solution.py:403
  53.4 1.6 %collective-permute-done.9.refs_3_ = f32[5,24,128]{2,1,0:T(8,128)S(1)} collective-permute-done((f32[5,24,128]{2,1,0:T(8,128)S(1)}, f32[5,24,128]{2,1,0:T(8,128)S(1)}, u32[]{:S(2)}, u32[]{:S(2)}) %collective-permute-start.9) | collective-permute-done | bytes 61472 | tf_op jit(solution)/shard_map/ppermute | solution.py:403
  55.0 0.0 collective-permute-done.8.refs_2_
  55.0 0.6 %collective-permute-done.7.refs_1_ = f32[5,24,128]{2,1,0:T(8,128)S(1)} collective-permute-done((f32[5,24,128]{2,1,0:T(8,128)S(1)}, f32[5,24,128]{2,1,0:T(8,128)S(1)}, u32[]{:S(2)}, u32[]{:S(2)}) %collective-permute-start.7) | collective-permute-done | bytes 61472 | tf_op jit(solution)/shard_map/ppermute | solution.py:403
  55.6 0.7 %place.1 = f32[5,96,128]{2,1,0:T(8,128)} custom-call(f32[5,24,128]{2,1,0:T(8,128)S(1)} %join.1.refs_0_, f32[5,24,128]{2,1,0:T(8,128)S(1)} %collective-permute-done.7.refs_1_, f32[5,24,128]{2,1,0:T(8,128)S(1)} %collective-permute-done.8.refs_2_, f32[5,24,128]{2,1,0:T(8,128)S(1)} %collective-permute-done.9.refs_3_), custom_call_target="tpu_custom_call" | custom-call | tf_op jit(solution)/shard_map/place/pallas_call | solution.py:539
  (1 shorter events, 0.0 us)
Async XLA Ops:
  0.0 13.3 %copy-start = (s32[96,128]{1,0:T(8,128)S(1)}, s32[96,128]{1,0:T(8,128)}, u32[]{:S(2)}) copy-start(s32[96,128]{1,0:T(8,128)} %cls_ref.3) | copy-start | bytes 147460
  8.0 13.6 %collective-permute-start = (f32[392,128]{1,0:T(8,128)S(1)}, f32[392,128]{1,0:T(8,128)S(1)}, u32[]{:S(2)}, u32[]{:S(2)}) collective-permute-start(f32[392,128]{1,0:T(8,128)S(1)} %get-tuple-element.15), channel_id=1, source_target_pairs={{0,1},{1,0},{2,3},{3,2},{4,5},{5,4},{6,7},{7,6},{8,9},{9,8},{10,11... | collective-permute-start | bytes 602120 | tf_op jit(solution)/shard_map/ppermute | solution.py:464
  8.6 13.0 %collective-permute-start.1 = (f32[392,128]{1,0:T(8,128)S(1)}, f32[392,128]{1,0:T(8,128)S(1)}, u32[]{:S(2)}, u32[]{:S(2)}) collective-permute-start(f32[392,128]{1,0:T(8,128)S(1)} %get-tuple-element.16), channel_id=1, source_target_pairs={{0,7},{1,2},{2,1},{3,4},{4,3},{5,6},{6,5},{7,0},{8,15},{9,10},{10,... | collective-permute-start | bytes 602120 | tf_op jit(solution)/shard_map/ppermute | solution.py:463
  13.3 8.3 %copy-start.2 = (s32[768]{0:T(1024)S(1)}, s32[768]{0:T(1024)}, u32[]{:S(2)}) copy-start(s32[768]{0:T(1024)} %param.7) | copy-start | bytes 9220
  13.3 8.3 %copy-start.3 = (f32[768]{0:T(1024)S(1)}, f32[768]{0:T(1024)}, u32[]{:S(2)}) copy-start(f32[768]{0:T(1024)} %param.8) | copy-start | bytes 9220
  21.6 12.3 %copy-start.1 = (f32[96,128]{1,0:T(8,128)S(1)}, f32[96,128]{1,0:T(8,128)}, u32[]{:S(2)}) copy-start(f32[96,128]{1,0:T(8,128)} %ann_ref.1) | copy-start | bytes 147460
  27.9 5.9 %collective-permute-start.3 = (f32[32,768]{1,0:T(8,128)S(1)}, f32[32,768]{1,0:T(8,128)S(1)}, u32[]{:S(2)}, u32[]{:S(2)}) collective-permute-start(f32[32,768]{1,0:T(8,128)S(1)} %get-tuple-element.19.loss_ref), channel_id=1, source_target_pairs={{0,7},{1,2},{2,1},{3,4},{4,3},{5,6},{6,5},{7,0},{8,15},{9,10},{10,... | collective-permute-start | bytes 294920 | tf_op jit(solution)/shard_map/ppermute | solution.py:463
  28.0 5.8 %collective-permute-start.2 = (f32[32,768]{1,0:T(8,128)S(1)}, f32[32,768]{1,0:T(8,128)S(1)}, u32[]{:S(2)}, u32[]{:S(2)}) collective-permute-start(f32[32,768]{1,0:T(8,128)S(1)} %get-tuple-element.19.loss_ref), channel_id=1, source_target_pairs={{0,1},{1,0},{2,3},{3,2},{4,5},{5,4},{6,7},{7,6},{8,9},{9,8},{10,11... | collective-permute-start | bytes 294920 | tf_op jit(solution)/shard_map/ppermute | solution.py:464
  40.4 4.6 %collective-permute-start.4 = (f32[7,24,128]{2,1,0:T(8,128)S(1)}, f32[7,24,128]{2,1,0:T(8,128)S(1)}, u32[]{:S(2)}, u32[]{:S(2)}) collective-permute-start(f32[7,24,128]{2,1,0:T(8,128)S(1)} %get-tuple-element.22), channel_id=1, source_target_pairs={{0,8},{8,0},{16,24},{24,16},{1,9},{9,1},{17,25},{25,17},{2,10},{10... | collective-permute-start | bytes 258056 | tf_op jit(solution)/shard_map/ppermute | solution.py:403
  42.0 4.5 %collective-permute-start.5 = (f32[7,24,128]{2,1,0:T(8,128)S(1)}, f32[7,24,128]{2,1,0:T(8,128)S(1)}, u32[]{:S(2)}, u32[]{:S(2)}) collective-permute-start(f32[7,24,128]{2,1,0:T(8,128)S(1)} %get-tuple-element.23), channel_id=1, source_target_pairs={{0,16},{8,24},{16,0},{24,8},{1,17},{9,25},{17,1},{25,9},{2,18},{10... | collective-permute-start | bytes 258056 | tf_op jit(solution)/shard_map/ppermute | solution.py:403
  43.5 6.3 %collective-permute-start.6 = (f32[7,24,128]{2,1,0:T(8,128)S(1)}, f32[7,24,128]{2,1,0:T(8,128)S(1)}, u32[]{:S(2)}, u32[]{:S(2)}) collective-permute-start(f32[7,24,128]{2,1,0:T(8,128)S(1)} %get-tuple-element.24), channel_id=1, source_target_pairs={{0,24},{8,16},{16,8},{24,0},{1,25},{9,17},{17,9},{25,1},{2,26},{10... | collective-permute-start | bytes 258056 | tf_op jit(solution)/shard_map/ppermute | solution.py:403
  49.8 5.2 %collective-permute-start.9 = (f32[5,24,128]{2,1,0:T(8,128)S(1)}, f32[5,24,128]{2,1,0:T(8,128)S(1)}, u32[]{:S(2)}, u32[]{:S(2)}) collective-permute-start(f32[5,24,128]{2,1,0:T(8,128)S(1)} %join.1.refs_0_), channel_id=1, source_target_pairs={{0,24},{8,16},{16,8},{24,0},{1,25},{9,17},{17,9},{25,1},{2,26},{10... | collective-permute-start | bytes 184328 | tf_op jit(solution)/shard_map/ppermute | solution.py:403
  49.9 5.1 %collective-permute-start.8 = (f32[5,24,128]{2,1,0:T(8,128)S(1)}, f32[5,24,128]{2,1,0:T(8,128)S(1)}, u32[]{:S(2)}, u32[]{:S(2)}) collective-permute-start(f32[5,24,128]{2,1,0:T(8,128)S(1)} %join.1.refs_0_), channel_id=1, source_target_pairs={{0,16},{8,24},{16,0},{24,8},{1,17},{9,25},{17,1},{25,9},{2,18},{10... | collective-permute-start | bytes 184328 | tf_op jit(solution)/shard_map/ppermute | solution.py:403
  51.4 4.2 %collective-permute-start.7 = (f32[5,24,128]{2,1,0:T(8,128)S(1)}, f32[5,24,128]{2,1,0:T(8,128)S(1)}, u32[]{:S(2)}, u32[]{:S(2)}) collective-permute-start(f32[5,24,128]{2,1,0:T(8,128)S(1)} %join.1.refs_0_), channel_id=1, source_target_pairs={{0,8},{8,0},{16,24},{24,16},{1,9},{9,1},{17,25},{25,17},{2,10},{10... | collective-permute-start | bytes 184328 | tf_op jit(solution)/shard_map/ppermute | solution.py:403

commit v4 on v3

--- a/solution.py
+++ b/solution.py
@@ -10,6 +10,7 @@
 ROW_REACH = 8
 TIME_STEP = 0.25
 CORIOLIS = 0.2
+HALF_STEP = 0.5 * TIME_STEP
 GROUP = 16
 EDGE = 4
 ZEROS = 8
@@ -33,14 +34,21 @@
     return lax.broadcasted_iota(jnp.int32, shape, len(shape) - 1)
 
 
+def packed_lanes(shape):
+    return (lanes_of(shape) + HALF) & (shape[-1] - 1)
+
+
 def roll_lanes(x, shift):
+    if isinstance(shift, int) and shift % x.shape[-1] == 0:
+        return x
     return pltpu.roll(x, shift % x.shape[-1] if isinstance(shift, int) else shift, x.ndim - 1)
 
 
 def shift_table(cols):
     k = lax.broadcasted_iota(jnp.int32, (2 * cols, cols), 0) & (cols - 1)
     c = lax.broadcasted_iota(jnp.int32, (2 * cols, cols), 1)
-    return (jnp.where(k == c + 1, 1.0, 0.0) - jnp.where(k == c - 1, 1.0, 0.0)).astype(bf16)
+    last = cols - 1
+    return (jnp.where(k == ((c + 1) & last), HALF_STEP, 0.0) - jnp.where(k == ((c - 1) & last), HALF_STEP, 0.0)).astype(bf16)
 
 
 def step(fields, depth, pad, slot, table):
@@ -58,12 +66,14 @@
     hi = both.astype(bf16)
     mid = (both - hi.astype(f32)).astype(bf16)
     slopes = jnp.dot(jnp.concatenate([hi, mid], axis=1), table[...], preferred_element_type=f32)
-    half = 0.5 * TIME_STEP
-    un = u - half * cols(h) + TIME_STEP * CORIOLIS * v
-    vn = v - half * rws(h, 0) - TIME_STEP * CORIOLIS * u
-    hn = h - half * (cols(depth * un) + rws(depth * vn, 1))
-    an = a - half * (un * slopes[:rows] + vn * rws(a, 2))
-    bn = b - half * (un * slopes[rows:] + vn * rws(b, 3))
+    turn = TIME_STEP * CORIOLIS
+    hs = HALF_STEP * h
+    un = u - cols(hs) + turn * v
+    vn = v - rws(hs, 0) - turn * u
+    hn = h - (cols(depth * un) + rws(depth * vn, 1))
+    vs = HALF_STEP * vn
+    an = a - (un * slopes[:rows] + vs * rws(a, 2))
+    bn = b - (un * slopes[rows:] + vs * rws(b, 3))
     return hn, un, vn, an, bn
 
 
@@ -86,10 +96,15 @@
     copies = [pltpu.make_async_copy(x_hbm.at[:, f], buf.at[f], sem.at[f]) for f in range(fields)]
     copies.append(pltpu.make_async_copy(cls_hbm, cls_ref, sem.at[fields]))
     copies.append(pltpu.make_async_copy(idx_hbm, idx_ref, sem.at[fields + 1]))
-    for c in copies:
-        c.start()
-
-    lane = lanes_of((8, cols))
+    for n in (0, 1, fields, fields + 1):
+        copies[n].start()
+
+    def arrive(f):
+        copies[f].wait()
+        if f + 2 < fields:
+            copies[f + 2].start()
+
+    lane = packed_lanes((8, cols))
     grp = lane // GROUP
     sub = (lane % GROUP) // EDGE
     jj = lane % EDGE
@@ -105,7 +120,7 @@
         for q in range(planes):
             acc = None
             for i in range(per):
-                r = roll_lanes(buf[f, q * per + i, at, :], GROUP * i + HALF)
+                r = roll_lanes(buf[f, q * per + i, at, :], GROUP * i)
                 acc = r if acc is None else jnp.where(grp == i, r, acc)
             g_ref[q, f, at, :] = acc
             r = roll_lanes(acc, EDGE * q - EDGE)
@@ -115,7 +130,7 @@
         return right, left
 
     for f in range(3):
-        copies[f].wait()
+        arrive(f)
         if f == 1:
             copies[fields].wait()
 
@@ -124,15 +139,15 @@
             if f == 1:
                 d = depth_of(cls_ref[pl.ds(t * 8, 8), :])
                 for n in range(3):
-                    e = roll_lanes(d, 3 * n + 3)
+                    e = roll_lanes(d, 3 * n + 3 - HALF)
                     right = jnp.where(lane == EDGE * n, e, right)
                     left = jnp.where(lane == EDGE * n + 3, e, left)
             put(f, t, right, left)
             return carry
 
         lax.fori_loop(0, rows // 8, body, 0, unroll=4)
-    copies[3].wait()
-    copies[4].wait()
+    arrive(3)
+    arrive(4)
 
     def tracers(t, carry):
         ra, la = edges(3, t)
@@ -149,8 +164,8 @@
 
 
 def forecast_kernel(x_ref, cls_ref, o_ref, pad, table):
-    depth = depth_of(cls_ref[...])
-    pl.when(pl.program_id(0) == 0)(lambda: prepare(pad, table))
+    depth = HALF_STEP * depth_of(cls_ref[...])
+    prepare(pad, table)
 
     def body(m, carry):
         out = two_steps([x_ref[f, m] for f in range(5)], depth, pad, table)
@@ -158,7 +173,7 @@
             o_ref[m, f] = out[f]
         return carry
 
-    lax.fori_loop(0, o_ref.shape[0], body, 0, unroll=4)
+    lax.fori_loop(0, o_ref.shape[0], body, 0, unroll=2)
 
 
 def pieces_of(x):
@@ -179,24 +194,30 @@
     planes = members // per
     even = lax.rem(lax.axis_index("col"), 2) == 0
     lane = lanes_of((rows, cols))
-    j = lane % GROUP
-    grp = lane // GROUP
+    place = packed_lanes((rows, cols))
+    j = place % GROUP
+    grp = place // GROUP
 
     def received(plane):
         at = slice(plane * rows, (plane + 1) * rows)
         a, b = ra_ref[at, :], rb_ref[at, :]
         return jnp.where(even, b, a), jnp.where(even, a, b)
 
-    depth = depth_of(cls_ref[...])
+    depth = HALF_STEP * depth_of(cls_ref[...])
     tiled = None
     for i in range(per):
-        r = roll_lanes(depth, GROUP * i + HALF)
+        r = roll_lanes(depth, GROUP * i)
         tiled = r if tiled is None else jnp.where(grp == i, r, tiled)
     ul, ur = received(1)
+
+    def lane_at(x, n):
+        at = (n - HALF) % cols
+        return x[:, at : at + 1]
+
     dl = dr = tiled
     for n in range(3):
-        dl = jnp.where(j == EDGE + n + 1, jnp.broadcast_to(ul[:, EDGE * n : EDGE * n + 1], dl.shape), dl)
-        dr = jnp.where(j == HALF + n, jnp.broadcast_to(ur[:, EDGE * n + 3 : EDGE * n + 4], dr.shape), dr)
+        dl = jnp.where(j == EDGE + n + 1, HALF_STEP * jnp.broadcast_to(lane_at(ul, EDGE * n), dl.shape), dl)
+        dr = jnp.where(j == HALF + n, HALF_STEP * jnp.broadcast_to(lane_at(ur, EDGE * n + 3), dr.shape), dr)
     xs[0, 5] = dl
     xs[1, 5] = dr
     for f in range(5):
@@ -239,7 +260,7 @@
     def split(q, carry):
         for i in range(0, per, 2):
             pair = [
-                jnp.where(border, roll_lanes(z_ref[q, 0], cols - HALF - GROUP * n), x_ref[q * per + n, 0])
+                jnp.where(border, roll_lanes(z_ref[q, 0], cols - GROUP * n), x_ref[q * per + n, 0])
                 for n in (i, i + 1)
             ]
             at = pl.ds(pl.multiple_of((q * per + i) * band, 16), 2 * band)
@@ -357,14 +378,14 @@
         return peak
 
     peak = lax.fori_loop(0, members // bufs.shape[0], smooth, jnp.full((rows, cols), -jnp.inf, f32))
-    tot[fields + 1] = peak
+    tot[fields] = peak
     lane = lanes_of((8, cols))
-    grp = lane // GROUP
+    grp = packed_lanes((8, cols)) // GROUP
     border = (lane < EDGE) | (lane >= cols - EDGE)
 
     def sums(t, carry):
         at = pl.ds(pl.multiple_of(t * 8, 8), 8)
-        top = tot[fields + 1, at, :]
+        top = tot[fields, at, :]
         total = jnp.zeros((8, cols), f32)
         s = [jnp.zeros((8, cols), f32)] * fields
         e = [jnp.zeros((8, cols), f32)] * fields
@@ -376,15 +397,16 @@
                 total = total + w
                 for f in range(fields):
                     s[f] = s[f] + w * x_ref[m, f, at, :]
-                r = roll_lanes(w, GROUP * i + HALF)
+                r = roll_lanes(w, GROUP * i)
                 packed = r if packed is None else jnp.where(grp == i, r, packed)
             for f in range(fields):
                 e[f] = e[f] + packed * z_ref[q, f, at, :]
+        inverse = 1.0 / total
         for f in range(fields):
             for k in (cols // 2, cols // 4, cols // 8):
                 e[f] = e[f] + roll_lanes(e[f], k)
-            tot[f, at, :] = jnp.where(border, roll_lanes(e[f], cols - HALF), s[f])
-        tot[fields, at, :] = total
+            tot[f, at, :] = jnp.where(border, e[f], s[f]) * inverse
+        tot[fields, at, :] = top + jnp.log(total)
         return carry
 
     lax.fori_loop(0, rows // 8, sums, 0, unroll=2)
@@ -406,12 +428,12 @@
 def join_kernel(*refs):
     *ins, out = refs
     fields = out.shape[0]
-    peak = functools.reduce(jnp.maximum, [r[fields + 1] for r in ins])
+    peak = functools.reduce(jnp.maximum, [r[fields] for r in ins])
     total = 0.0
     s = [0.0] * fields
     for r in ins:
-        e = jnp.exp(r[fields + 1] - peak)
-        total = total + r[fields] * e
+        e = jnp.exp(r[fields] - peak)
+        total = total + e
         for f in range(fields):
             s[f] = s[f] + r[f] * e
     for f in range(fields):
@@ -465,16 +487,11 @@
         return ra, rb
 
     ra, rb = exchange(pa, pb)
-    block = 4
     raw = pl.pallas_call(
         forecast_kernel,
         out_shape=S(ensemble.shape, f32),
-        grid=(members // block,),
-        in_specs=[
-            pl.BlockSpec((fields, block, rows, cols), lambda m: (0, m, 0, 0)),
-            pl.BlockSpec((rows, cols), lambda m: (0, 0)),
-        ],
-        out_specs=pl.BlockSpec((block, fields, rows, cols), lambda m: (m, 0, 0, 0)),
+        in_specs=[VMEM, VMEM],
+        out_specs=VMEM,
         scratch_shapes=[pltpu.VMEM((8, rows + 2 * ZEROS, cols), f32), pltpu.VMEM((2 * cols, cols), bf16)],
         compiler_params=params(12),
         name="forecast",
@@ -508,7 +525,7 @@
         name="own",
     )(loss, idx)
 
-    part = S((fields + 2, rows // ndom, cols), f32)
+    part = S((fields + 1, rows // ndom, cols), f32)
     sums = pl.pallas_call(
         functools.partial(weigh_kernel, radius=radius, parts=ndom),
         out_shape=(part,) * ndom,
@@ -519,14 +536,14 @@
             pltpu.VMEM((2, BANDS * cols // 2, nobs), bf16),
             pltpu.VMEM((2, tall, BANDS * cols // 2), f32),
             pltpu.VMEM((members, rows, cols), f32),
-            pltpu.VMEM((fields + 2, rows, cols), f32),
+            pltpu.VMEM((fields + 1, rows, cols), f32),
             pltpu.VMEM((4, 4, rows + 4 * ZEROS, cols), f32),
         ],
         compiler_params=params(30),
         name="weigh",
     )(own, la, lb, ra, rb, raw, edges, annealing_exponents)
 
-    parts = [sums[0]] + [swap(sums[k], k, ndom) for k in range(1, ndom)]
+    parts = [swap(sums[k], k, ndom) if k else sums[0] for k in range(ndom - 1, -1, -1)]
     mine = pl.pallas_call(
         join_kernel,
         out_shape=S((fields, rows // ndom, cols), f32),

time: 56.5 us -> 52.7 us (0.933)
  Pallas kernels: 32 us -> 28.9 us
  waiting for transfers between devices: 11.8 us -> 11 us
    pallas_call x1, Pallas kernels: 8.29 us -> 6.87 us  [on_device(): pl.pallas_call(forecast_kernel, out_shape=S(ensemble.shape, f32), in_spec...]
    pallas_call x1, Pallas kernels: 7.98 us -> 6.92 us  [on_device(): pl.pallas_call(pack_kernel, out_shape=(S((planes, fields, rows, cols), f3...]
    ppermute x6, waiting for transfers between devices: 8.07 us -> 7.27 us  [swap(): lax.ppermute(x, 'dom', [(i, i ^ k if count & count - 1 == 0 else (i + k)...]
  transfers between devices with their start and end apart: 10 -> 10, of which waited for: 6 -> 6; matrix products, arithmetic and copies ran while one was open for 0% -> 0% of each run, Pallas kernels for 18% -> 17%
where the time goes in v4:
time: 52.7 us; the launch traced here: 52.5 us
  Pallas kernels  28.9 us (55%)
  starting transfers between devices  12.5 us (24%)
  waiting for transfers between devices  11 us (21%)
    ppermute x6, waiting for transfers between devices, swap(): lax.ppermute(x, 'dom', [(i, i ^ k if count & count - 1 == 0 else (i + k)...  7.27 us
    ppermute x6, starting transfers between devices, swap(): lax.ppermute(x, 'dom', [(i, i ^ k if count & count - 1 == 0 else (i + k)...  7.11 us
    pallas_call x1, Pallas kernels, on_device(): pl.pallas_call(pack_kernel, out_shape=(S((planes, fields, rows, cols), f3...  6.92 us
    pallas_call x1, Pallas kernels, on_device(): pl.pallas_call(forecast_kernel, out_shape=S(ensemble.shape, f32), in_spec...  6.87 us
    pallas_call x1, Pallas kernels, on_device(): pl.pallas_call(edge_kernel, out_shape=(S((planes, fields, rows, cols), f3...  6.2 us
    pallas_call x1, Pallas kernels, on_device(): pl.pallas_call(functools.partial(weigh_kernel, radius=radius, parts=ndom)...  6.12 us
    ppermute x2, starting transfers between devices, exchange(): rb = lax.ppermute(b, 'col', outer)  4.77 us
    ppermute x2, waiting for transfers between devices, exchange(): rb = lax.ppermute(b, 'col', outer)  3.7 us
  transfers between devices with their start and end apart: 10, of which 6 were waited for; matrix products, arithmetic and copies ran while one was open for 0% of the time, Pallas kernels for 17%

profile of v4, /device:TPU:0, one launch (start us, length us, event | category | flops | bytes accessed | tf_op | source)
XLA Modules:
  0.0 52.5 jit_solution(16836740045793952428)
XLA Ops:
  0.0 0.0 copy-start
  0.0 6.9 %pack.1 = (f32[4,5,96,128]{3,2,1,0:T(8,128)S(1)}, f32[392,128]{1,0:T(8,128)S(1)}, f32[392,128]{1,0:T(8,128)S(1)}, f32[5,32,96,128]{3,2,1,0:T(8,128)S(1)}) custom-call(f32[32,5,96,128]{3,2,1,0:T(8,128)} %x_hbm.1, s32[96,128]{1,0:T(8,128)} %cls_ref.3, s32[6,128]{1,0:T(8,128)} %bitcast.2), custom_call_target="tpu_custom_call" | custom-call | tf_op jit(solution)/shard_map/pack/pallas_call | solution.py:467
  6.9 0.6 %collective-permute-start = (f32[392,128]{1,0:T(8,128)S(1)}, f32[392,128]{1,0:T(8,128)S(1)}, u32[]{:S(2)}, u32[]{:S(2)}) collective-permute-start(f32[392,128]{1,0:T(8,128)S(1)} %get-tuple-element.15), channel_id=1, source_target_pairs={{0,1},{1,0},{2,3},{3,2},{4,5},{5,4},{6,7},{7,6},{8,9},{9,8},{10,11... | collective-permute-start | bytes 602120 | tf_op jit(solution)/shard_map/ppermute | solution.py:486
  7.5 4.7 %collective-permute-start.1 = (f32[392,128]{1,0:T(8,128)S(1)}, f32[392,128]{1,0:T(8,128)S(1)}, u32[]{:S(2)}, u32[]{:S(2)}) collective-permute-start(f32[392,128]{1,0:T(8,128)S(1)} %get-tuple-element.16), channel_id=1, source_target_pairs={{0,7},{1,2},{2,1},{3,4},{4,3},{5,6},{6,5},{7,0},{8,15},{9,10},{10,... | collective-permute-start | bytes 602120 | tf_op jit(solution)/shard_map/ppermute | solution.py:485
  12.2 0.0 copy-done
  12.2 0.0 copy-start.2
  12.2 0.0 copy-start.3
  12.2 6.9 %forecast.1.x_ref = f32[32,5,96,128]{3,2,1,0:T(8,128)S(1)} custom-call(f32[5,32,96,128]{3,2,1,0:T(8,128)S(1)} %get-tuple-element.18.x_ref, s32[96,128]{1,0:T(8,128)S(1)} %copy-done), custom_call_target="tpu_custom_call" | custom-call | tf_op jit(solution)/shard_map/forecast/pallas_call | solution.py:490
  19.1 0.0 copy-start.1
  19.1 0.0 collective-permute-done.ra_ref
  19.1 0.0 collective-permute-done.1.rb_ref
  19.1 0.0 copy-done.2
  19.1 0.0 copy-done.3
  19.1 6.2 %edges.1 = (f32[4,5,96,128]{3,2,1,0:T(8,128)S(1)}, f32[32,768]{1,0:T(8,128)S(1)}) custom-call(f32[392,128]{1,0:T(8,128)S(1)} %collective-permute-done.ra_ref, f32[392,128]{1,0:T(8,128)S(1)} %collective-permute-done.1.rb_ref, f32[4,5,96,128]{3,2,1,0:T(8,128)S(1)} %get-tuple-element.17.g_ref, s32[96,128]{1,0:T(8,128)S(1)} %copy-done, ...), custom_call_target="tpu_custom_call" | custom-call | tf_op jit(solution)/shard_map/edges/pallas_call | solution.py:500
  25.3 0.1 collective-permute-start.3
  25.4 0.1 collective-permute-start.2
  25.5 2.0 %own.1.own_ref = f32[768,512]{1,0:T(8,128)S(1)} custom-call(f32[32,768]{1,0:T(8,128)S(1)} %get-tuple-element.19.loss_ref, s32[6,128]{1,0:T(8,128)S(1)} %bitcast.4), custom_call_target="tpu_custom_call" | custom-call | tf_op jit(solution)/shard_map/own/pallas_call | solution.py:518
  27.5 3.7 %collective-permute-done.3.lb_ref = f32[32,768]{1,0:T(8,128)S(1)} collective-permute-done((f32[32,768]{1,0:T(8,128)S(1)}, f32[32,768]{1,0:T(8,128)S(1)}, u32[]{:S(2)}, u32[]{:S(2)}) %collective-permute-start.3) | collective-permute-done | bytes 98336 | tf_op jit(solution)/shard_map/ppermute | solution.py:485
  31.2 0.0 collective-permute-done.2.la_ref
  31.2 0.0 copy-done.1
  31.2 6.1 %weigh.1 = (f32[6,24,128]{2,1,0:T(8,128)S(1)}, f32[6,24,128]{2,1,0:T(8,128)S(1)}, f32[6,24,128]{2,1,0:T(8,128)S(1)}, f32[6,24,128]{2,1,0:T(8,128)S(1)}) custom-call(f32[768,512]{1,0:T(8,128)S(1)} %own.1.own_ref, f32[32,768]{1,0:T(8,128)S(1)} %collective-permute-done.2.la_ref, f32[32,768]{1,0:T(8,128)S(1)} %collective-permute-done.3.lb_ref, ...), custom_call_target="tpu_custom_call" | custom-call | tf_op jit(solution)/shard_map/weigh/pallas_call | solution.py:529
  37.4 2.5 %collective-permute-start.4 = (f32[6,24,128]{2,1,0:T(8,128)S(1)}, f32[6,24,128]{2,1,0:T(8,128)S(1)}, u32[]{:S(2)}, u32[]{:S(2)}) collective-permute-start(f32[6,24,128]{2,1,0:T(8,128)S(1)} %get-tuple-element.21), channel_id=1, source_target_pairs={{0,24},{8,16},{16,8},{24,0},{1,25},{9,17},{17,9},{25,1},{2,26},{10... | collective-permute-start | bytes 221192 | tf_op jit(solution)/shard_map/ppermute | solution.py:425
  39.9 0.5 collective-permute-start.5
  40.4 0.5 %collective-permute-start.6 = (f32[6,24,128]{2,1,0:T(8,128)S(1)}, f32[6,24,128]{2,1,0:T(8,128)S(1)}, u32[]{:S(2)}, u32[]{:S(2)}) collective-permute-start(f32[6,24,128]{2,1,0:T(8,128)S(1)} %get-tuple-element.23), channel_id=1, source_target_pairs={{0,8},{8,0},{16,24},{24,16},{1,9},{9,1},{17,25},{25,17},{2,10},{10... | collective-permute-start | bytes 221192 | tf_op jit(solution)/shard_map/ppermute | solution.py:425
  40.9 1.8 %collective-permute-done.4.refs_0_ = f32[6,24,128]{2,1,0:T(8,128)S(1)} collective-permute-done((f32[6,24,128]{2,1,0:T(8,128)S(1)}, f32[6,24,128]{2,1,0:T(8,128)S(1)}, u32[]{:S(2)}, u32[]{:S(2)}) %collective-permute-start.4) | collective-permute-done | bytes 73760 | tf_op jit(solution)/shard_map/ppermute | solution.py:425
  42.7 2.9 %collective-permute-done.5.refs_1_ = f32[6,24,128]{2,1,0:T(8,128)S(1)} collective-permute-done((f32[6,24,128]{2,1,0:T(8,128)S(1)}, f32[6,24,128]{2,1,0:T(8,128)S(1)}, u32[]{:S(2)}, u32[]{:S(2)}) %collective-permute-start.5) | collective-permute-done | bytes 73760 | tf_op jit(solution)/shard_map/ppermute | solution.py:425
  45.6 0.0 collective-permute-done.6.refs_2_
  45.6 1.0 %collective-permute-start.9 = (f32[5,24,128]{2,1,0:T(8,128)S(1)}, f32[5,24,128]{2,1,0:T(8,128)S(1)}, u32[]{:S(2)}, u32[]{:S(2)}) collective-permute-start(f32[5,24,128]{2,1,0:T(8,128)S(1)} %join.1.refs_0_), channel_id=1, source_target_pairs={{0,24},{8,16},{16,8},{24,0},{1,25},{9,17},{17,9},{25,1},{2,26},{10... | collective-permute-start | bytes 184328 | tf_op jit(solution)/shard_map/ppermute | solution.py:425
  46.6 1.0 %collective-permute-start.8 = (f32[5,24,128]{2,1,0:T(8,128)S(1)}, f32[5,24,128]{2,1,0:T(8,128)S(1)}, u32[]{:S(2)}, u32[]{:S(2)}) collective-permute-start(f32[5,24,128]{2,1,0:T(8,128)S(1)} %join.1.refs_0_), channel_id=1, source_target_pairs={{0,16},{8,24},{16,0},{24,8},{1,17},{9,25},{17,1},{25,9},{2,18},{10... | collective-permute-start | bytes 184328 | tf_op jit(solution)/shard_map/ppermute | solution.py:425
  47.6 1.6 %collective-permute-start.7 = (f32[5,24,128]{2,1,0:T(8,128)S(1)}, f32[5,24,128]{2,1,0:T(8,128)S(1)}, u32[]{:S(2)}, u32[]{:S(2)}) collective-permute-start(f32[5,24,128]{2,1,0:T(8,128)S(1)} %join.1.refs_0_), channel_id=1, source_target_pairs={{0,8},{8,0},{16,24},{24,16},{1,9},{9,1},{17,25},{25,17},{2,10},{10... | collective-permute-start | bytes 184328 | tf_op jit(solution)/shard_map/ppermute | solution.py:425
  49.2 1.7 %collective-permute-done.9.refs_3_ = f32[5,24,128]{2,1,0:T(8,128)S(1)} collective-permute-done((f32[5,24,128]{2,1,0:T(8,128)S(1)}, f32[5,24,128]{2,1,0:T(8,128)S(1)}, u32[]{:S(2)}, u32[]{:S(2)}) %collective-permute-start.9) | collective-permute-done | bytes 61472 | tf_op jit(solution)/shard_map/ppermute | solution.py:425
  50.9 0.5 %collective-permute-done.8.refs_2_ = f32[5,24,128]{2,1,0:T(8,128)S(1)} collective-permute-done((f32[5,24,128]{2,1,0:T(8,128)S(1)}, f32[5,24,128]{2,1,0:T(8,128)S(1)}, u32[]{:S(2)}, u32[]{:S(2)}) %collective-permute-start.8) | collective-permute-done | bytes 61472 | tf_op jit(solution)/shard_map/ppermute | solution.py:425
  51.4 0.4 collective-permute-done.7.refs_1_
  51.8 0.7 %place.1 = f32[5,96,128]{2,1,0:T(8,128)} custom-call(f32[5,24,128]{2,1,0:T(8,128)S(1)} %join.1.refs_0_, f32[5,24,128]{2,1,0:T(8,128)S(1)} %collective-permute-done.7.refs_1_, f32[5,24,128]{2,1,0:T(8,128)S(1)} %collective-permute-done.8.refs_2_, f32[5,24,128]{2,1,0:T(8,128)S(1)} %collective-permute-done.9.refs_3_), custom_call_target="tpu_custom_call" | custom-call | tf_op jit(solution)/shard_map/place/pallas_call | solution.py:556
  (1 shorter events, 0.0 us)
Async XLA Ops:
  0.0 12.2 %copy-start = (s32[96,128]{1,0:T(8,128)S(1)}, s32[96,128]{1,0:T(8,128)}, u32[]{:S(2)}) copy-start(s32[96,128]{1,0:T(8,128)} %cls_ref.3) | copy-start | bytes 147460
  6.9 12.2 %collective-permute-start = (f32[392,128]{1,0:T(8,128)S(1)}, f32[392,128]{1,0:T(8,128)S(1)}, u32[]{:S(2)}, u32[]{:S(2)}) collective-permute-start(f32[392,128]{1,0:T(8,128)S(1)} %get-tuple-element.15), channel_id=1, source_target_pairs={{0,1},{1,0},{2,3},{3,2},{4,5},{5,4},{6,7},{7,6},{8,9},{9,8},{10,11... | collective-permute-start | bytes 602120 | tf_op jit(solution)/shard_map/ppermute | solution.py:486
  7.5 11.6 %collective-permute-start.1 = (f32[392,128]{1,0:T(8,128)S(1)}, f32[392,128]{1,0:T(8,128)S(1)}, u32[]{:S(2)}, u32[]{:S(2)}) collective-permute-start(f32[392,128]{1,0:T(8,128)S(1)} %get-tuple-element.16), channel_id=1, source_target_pairs={{0,7},{1,2},{2,1},{3,4},{4,3},{5,6},{6,5},{7,0},{8,15},{9,10},{10,... | collective-permute-start | bytes 602120 | tf_op jit(solution)/shard_map/ppermute | solution.py:485
  12.2 6.9 %copy-start.2 = (s32[768]{0:T(1024)S(1)}, s32[768]{0:T(1024)}, u32[]{:S(2)}) copy-start(s32[768]{0:T(1024)} %param.7) | copy-start | bytes 9220
  12.2 6.9 %copy-start.3 = (f32[768]{0:T(1024)S(1)}, f32[768]{0:T(1024)}, u32[]{:S(2)}) copy-start(f32[768]{0:T(1024)} %param.8) | copy-start | bytes 9220
  19.1 12.2 %copy-start.1 = (f32[96,128]{1,0:T(8,128)S(1)}, f32[96,128]{1,0:T(8,128)}, u32[]{:S(2)}) copy-start(f32[96,128]{1,0:T(8,128)} %ann_ref.1) | copy-start | bytes 147460
  25.3 5.9 %collective-permute-start.3 = (f32[32,768]{1,0:T(8,128)S(1)}, f32[32,768]{1,0:T(8,128)S(1)}, u32[]{:S(2)}, u32[]{:S(2)}) collective-permute-start(f32[32,768]{1,0:T(8,128)S(1)} %get-tuple-element.19.loss_ref), channel_id=1, source_target_pairs={{0,7},{1,2},{2,1},{3,4},{4,3},{5,6},{6,5},{7,0},{8,15},{9,10},{10,... | collective-permute-start | bytes 294920 | tf_op jit(solution)/shard_map/ppermute | solution.py:485
  25.4 5.8 %collective-permute-start.2 = (f32[32,768]{1,0:T(8,128)S(1)}, f32[32,768]{1,0:T(8,128)S(1)}, u32[]{:S(2)}, u32[]{:S(2)}) collective-permute-start(f32[32,768]{1,0:T(8,128)S(1)} %get-tuple-element.19.loss_ref), channel_id=1, source_target_pairs={{0,1},{1,0},{2,3},{3,2},{4,5},{5,4},{6,7},{7,6},{8,9},{9,8},{10,11... | collective-permute-start | bytes 294920 | tf_op jit(solution)/shard_map/ppermute | solution.py:486
  37.4 5.3 %collective-permute-start.4 = (f32[6,24,128]{2,1,0:T(8,128)S(1)}, f32[6,24,128]{2,1,0:T(8,128)S(1)}, u32[]{:S(2)}, u32[]{:S(2)}) collective-permute-start(f32[6,24,128]{2,1,0:T(8,128)S(1)} %get-tuple-element.21), channel_id=1, source_target_pairs={{0,24},{8,16},{16,8},{24,0},{1,25},{9,17},{17,9},{25,1},{2,26},{10... | collective-permute-start | bytes 221192 | tf_op jit(solution)/shard_map/ppermute | solution.py:425
  39.9 5.7 %collective-permute-start.5 = (f32[6,24,128]{2,1,0:T(8,128)S(1)}, f32[6,24,128]{2,1,0:T(8,128)S(1)}, u32[]{:S(2)}, u32[]{:S(2)}) collective-permute-start(f32[6,24,128]{2,1,0:T(8,128)S(1)} %get-tuple-element.22), channel_id=1, source_target_pairs={{0,16},{8,24},{16,0},{24,8},{1,17},{9,25},{17,1},{25,9},{2,18},{10... | collective-permute-start | bytes 221192 | tf_op jit(solution)/shard_map/ppermute | solution.py:425
  40.4 5.2 %collective-permute-start.6 = (f32[6,24,128]{2,1,0:T(8,128)S(1)}, f32[6,24,128]{2,1,0:T(8,128)S(1)}, u32[]{:S(2)}, u32[]{:S(2)}) collective-permute-start(f32[6,24,128]{2,1,0:T(8,128)S(1)} %get-tuple-element.23), channel_id=1, source_target_pairs={{0,8},{8,0},{16,24},{24,16},{1,9},{9,1},{17,25},{25,17},{2,10},{10... | collective-permute-start | bytes 221192 | tf_op jit(solution)/shard_map/ppermute | solution.py:425
  45.6 5.3 %collective-permute-start.9 = (f32[5,24,128]{2,1,0:T(8,128)S(1)}, f32[5,24,128]{2,1,0:T(8,128)S(1)}, u32[]{:S(2)}, u32[]{:S(2)}) collective-permute-start(f32[5,24,128]{2,1,0:T(8,128)S(1)} %join.1.refs_0_), channel_id=1, source_target_pairs={{0,24},{8,16},{16,8},{24,0},{1,25},{9,17},{17,9},{25,1},{2,26},{10... | collective-permute-start | bytes 184328 | tf_op jit(solution)/shard_map/ppermute | solution.py:425
  46.6 4.9 %collective-permute-start.8 = (f32[5,24,128]{2,1,0:T(8,128)S(1)}, f32[5,24,128]{2,1,0:T(8,128)S(1)}, u32[]{:S(2)}, u32[]{:S(2)}) collective-permute-start(f32[5,24,128]{2,1,0:T(8,128)S(1)} %join.1.refs_0_), channel_id=1, source_target_pairs={{0,16},{8,24},{16,0},{24,8},{1,17},{9,25},{17,1},{25,9},{2,18},{10... | collective-permute-start | bytes 184328 | tf_op jit(solution)/shard_map/ppermute | solution.py:425
  47.6 4.2 %collective-permute-start.7 = (f32[5,24,128]{2,1,0:T(8,128)S(1)}, f32[5,24,128]{2,1,0:T(8,128)S(1)}, u32[]{:S(2)}, u32[]{:S(2)}) collective-permute-start(f32[5,24,128]{2,1,0:T(8,128)S(1)} %join.1.refs_0_), channel_id=1, source_target_pairs={{0,8},{8,0},{16,24},{24,16},{1,9},{9,1},{17,25},{25,17},{2,10},{10... | collective-permute-start | bytes 184328 | tf_op jit(solution)/shard_map/ppermute | solution.py:425
